TPU v7x, 32 devices: a whole 2x2x4 slice. The times are simulated.
32 devices in a mesh: cluster: 8 (over y, x, core), sample: 4 (over z).
Axes of the slice: x: 2, y: 2, z: 4, core: 2. Of those that a mesh axis runs over, the one named last changes fastest.
Arguments:
- child_pattern: float32 [2, 1024, 16384], P(None, 'cluster', 'sample'), may hold values from -6 to 6
- child_local: float32 [2, 1024, 16384], P(None, 'cluster', 'sample'), may hold values from -6 to 6
- interp_weight: float32 [6, 32768], P(None, 'sample'), may hold values from -0.1 to 0.3
- child_phase: float32 [8, 32768], P(None, 'sample'), may hold values from -3.140625 to 3.140625
- translator: float32 [316, 2, 32768], P(None, None, 'sample'), may hold values from -0.6 to 0.6
- partners: int32 [128, 64], replicated, may hold values from 0 to 127
- operator_id: int32 [128, 64], replicated, may hold values from 0 to 315
- list_len: int32 [128], replicated, may hold values from 8 to 64, as said below
Outputs:
- parent_incoming: float32 [2, 128, 32768], P(None, 'cluster', 'sample')
- child_incoming: float32 [2, 1024, 16384], P(None, 'cluster', 'sample')
Inputs may be any that keep to these rules, and one draw needn't show every extreme that they name: Parent q's interaction list is its first list_len[q] entries of partners and operator_id; later entries are unused.
All inputs are finite; a program needn't handle non-finite values.
Results may differ from a plain program's by a relative error of at most 0.0003.
Values sent between devices are 32-bit elements; how exact they have to be, the bound alone decides.
No kernel may reach another device: no remote copies, remote signals or barrier semaphores. Data moves between devices by JAX's collectives and lax.ppermute only.
A program may use at most 192 MiB of HBM per device.

v0:
```python
import jax
import jax.numpy as jnp
from jax import lax
from jax.sharding import PartitionSpec as P

TAPS = 6
CHILDREN = 8


def with_halo(block, sides, width):
    for axis, dim in sides:
        count = lax.axis_size(axis)
        forward = [(i, i + 1) for i in range(count - 1)]
        forward.append((count - 1, 0))
        backward = [(target, source) for source, target in forward]
        low = lax.ppermute(
            lax.slice_in_dim(block, block.shape[dim] - width, None, axis=dim), axis, forward
        )
        high = lax.ppermute(lax.slice_in_dim(block, 0, width, axis=dim), axis, backward)
        block = jnp.concatenate([low, block, high], axis=dim)
    return block


def translate(pattern, table, partner_rows, operator_rows, lengths):
    receivers = partner_rows.shape[0]
    slot_count = partner_rows.shape[1]
    group_size = 16
    sample_count = pattern.shape[2]

    def advance(block, total):
        partner_cols = lax.dynamic_slice_in_dim(partner_rows, block * group_size, group_size, 1)
        operator_cols = lax.dynamic_slice_in_dim(operator_rows, block * group_size, group_size, 1)
        slot_index = block * group_size + jnp.arange(group_size)
        alive_mask = (slot_index[None, :] < lengths[:, None]).astype(jnp.float32)
        source = jnp.take(pattern, partner_cols, axis=1)
        coupling = jnp.take(table, operator_cols, axis=0)
        coup_real = coupling[:, :, 0] * alive_mask[:, :, None]
        coup_imag = coupling[:, :, 1] * alive_mask[:, :, None]
        real_part = jnp.sum(coup_real * source[0] - coup_imag * source[1], axis=1)
        imag_part = jnp.sum(coup_real * source[1] + coup_imag * source[0], axis=1)
        return total + jnp.stack([real_part, imag_part])

    start_total = jnp.zeros((2, receivers, sample_count), jnp.float32)
    return lax.fori_loop(0, slot_count // group_size, advance, start_total)


def phase_sum(upsampled, cosine, sine, parent_count):
    grouped = upsampled.reshape(2, parent_count, CHILDREN, upsampled.shape[2])
    real_part = jnp.sum(cosine[None] * grouped[0] - sine[None] * grouped[1], axis=1)
    imag_part = jnp.sum(cosine[None] * grouped[1] + sine[None] * grouped[0], axis=1)
    return jnp.stack([real_part, imag_part])


def phase_spread(incoming, cosine, sine):
    shifted_real = cosine[None] * incoming[0][:, None] + sine[None] * incoming[1][:, None]
    shifted_imag = cosine[None] * incoming[1][:, None] - sine[None] * incoming[0][:, None]
    return jnp.stack([shifted_real, shifted_imag]).reshape(2, -1, incoming.shape[2])


def local(
    child_pattern,
    child_local,
    interp_weight,
    child_phase,
    translator,
    partners,
    operator_id,
    list_len,
):
    rim_width = TAPS // 2
    child_count = child_pattern.shape[1]
    parent_count = child_count // CHILDREN
    half_samples = child_pattern.shape[2]
    cosine = jnp.cos(child_phase)
    sine = jnp.sin(child_phase)
    cos_even = cosine[:, 0::2]
    cos_odd = cosine[:, 1::2]
    sin_even = sine[:, 0::2]
    sin_odd = sine[:, 1::2]
    weight_even = interp_weight[:, 0::2]
    weight_odd = interp_weight[:, 1::2]
    padded = with_halo(child_pattern, (("sample", 2),), rim_width)
    up_even = jnp.zeros((2, child_count, half_samples), jnp.float32)
    up_odd = jnp.zeros((2, child_count, half_samples), jnp.float32)
    for tap in range(TAPS):
        window = padded[:, :, 1 + tap : 1 + tap + half_samples]
        up_even = up_even + weight_even[tap][None, None, :] * window
        up_odd = up_odd + weight_odd[tap][None, None, :] * window
    parent_even = phase_sum(up_even, cos_even, sin_even, parent_count)
    parent_odd = phase_sum(up_odd, cos_odd, sin_odd, parent_count)
    parent = jnp.stack([parent_even, parent_odd], axis=3).reshape(2, parent_count, 2 * half_samples)
    cluster_index = lax.axis_index("cluster")
    whole = lax.all_gather(parent, "cluster", axis=1, tiled=True)
    first_row = cluster_index * parent_count
    own_partners = lax.dynamic_slice_in_dim(partners, first_row, parent_count, 0)
    own_operators = lax.dynamic_slice_in_dim(operator_id, first_row, parent_count, 0)
    own_lengths = lax.dynamic_slice_in_dim(list_len, first_row, parent_count, 0)
    incoming = translate(whole, translator, own_partners, own_operators, own_lengths)
    shift_even = phase_spread(incoming[:, :, 0::2], cos_even, sin_even)
    shift_odd = phase_spread(incoming[:, :, 1::2], cos_odd, sin_odd)
    weighted = jnp.stack(
        [
            weight_even[tap][None, None, :] * shift_even
            + weight_odd[tap][None, None, :] * shift_odd
            for tap in range(TAPS)
        ]
    )
    padded_weighted = with_halo(weighted, (("sample", 3),), rim_width)
    child_incoming = child_local
    for tap in range(TAPS):
        offset = 2 * rim_width - 1 - tap
        child_incoming = child_incoming + padded_weighted[tap, :, :, offset : offset + half_samples]
    return (incoming, child_incoming)


def solution(mesh):
    placed = (
        P(None, "cluster", "sample"),
        P(None, "cluster", "sample"),
        P(None, "sample"),
        P(None, "sample"),
        P(None, None, "sample"),
        P(),
        P(),
        P(),
    )
    return jax.shard_map(
        local,
        mesh=mesh,
        in_specs=placed,
        out_specs=(P(None, "cluster", "sample"), P(None, "cluster", "sample")),
        check_vma=False,
    )
```

profile of v0, /device:TPU:0, one launch (start us, length us, event | category | flops | bytes accessed | tf_op | source)
XLA Modules:
  0.0 765.8 jit_solution(4563911441418109952)
XLA Ops:
  8.3 3.1 collective-permute-start
  13.5 4.3 slice.209
  17.8 4.3 slice.191
  24.2 4.6 constant_dynamic-update-slice_fusion.1
  28.8 4.5 slice.208
  33.3 4.5 slice.190
  37.8 4.5 slice.217
  42.4 4.5 slice.206
  47.7 14.7 %multiply_add_fusion = f32[2,128,4096]{2,1,0:T(8,128)S(1)} fusion(f32[2,128,4096]{2,1,0:T(8,128)} %param.10, f32[2,128,4099]{2,1,0:T(8,128)} %constant_dynamic-update-slice_fusion, f32[2,128,3]{2,1,0:T(8,128)S(1)} %collective-permute-done, f32[4096]{0:T(1024)S(1)} %bitcast.173, f32[4096]{0:T(1024)S(1)} %bitcast.175, f32[4096]{0:T(1024)S(1)} %bitcast.177, ...), kind=kLoop, calls=%fused_computation.54 | loop fusion | flops 13631488 | bytes 21072896 | tf_op jit(solution)/shard_map/add | solution.py:88
  64.5 6.1 multiply_add_fusion.1
  72.3 8.0 %copy.48 = f32[2,16,4096,2]{1,3,2,0:T(2,128)} copy(f32[2,16,4096,2]{2,1,0,3:T(8,128)S(1)} %pad_maximum_fusion.5) | data formatting | bytes 2097152 | tf_op jit(solution)/shard_map/stack | solution.py:91
  80.3 6.1 copy.49
  86.7 53.8 %all-gather.2.cloned.1.call-done = f32[2,128,8192]{2,0,1:T(2,128)} async-done(((f32[2,16,8192]{2,0,1:T(2,128)}), f32[2,128,8192]{2,0,1:T(2,128)}) %all-gather.2.cloned.1.call-update) | async-done | bytes 8388624 | tf_op jit(solution)/shard_map/all_gather | solution.py:93
  140.5 532.0 %while.14 = (s32[]{:T(128)}, f32[2,16,8192]{2,1,0:T(8,128)S(1)}, s32[16,64]{0,1:T(8,128)S(1)}, f32[316,2,8192]{2,1,0:T(2,128)}, s32[16]{0:T(128)S(1)}, /*index=5...) while((s32[]{:T(128)}, f32[2,16,8192]{2,1,0:T(8,128)S(1)}, ...), condition=%wide.region_7.8_spmd.clone, body=%wide.region_4.7_spmd.clone.sunk | while | flops 29891604 | bytes 205555056 | solution.py:44
  141.1 29.8 %gather_fusion.1 = f32[256,2,8192]{2,1,0:T(2,128)} fusion(f32[316,2,8192]{2,1,0:T(2,128)} %get-tuple-element.298, s32[1024]{0:T(1024)S(1)} %pad_clamp_fusion.5), kind=kCustom, calls=%fused_computation.clone.clone.1 | custom fusion | bytes 33555456 | tf_op jit(solution)/shard_map/while/body/eval_jaxpr/jit(_take)/gather | solution.py:36
  170.9 18.0 %copy_select_fusion.2 = f32[16,16,2,8192]{3,1,0,2:T(8,128)} fusion(f32[16,16,2,8192]{3,2,1,0:T(2,128)} %bitcast.156, pred[16,16]{1,0:T(8,128)(4,1)S(1)} %compare_and_fusion.5), kind=kLoop, calls=%fused_computation.2.clone.1 | loop fusion | flops 4194304 | bytes 33554688 | tf_op jit(solution)/shard_map/while/body/eval_jaxpr/jit(_take)/select_n | solution.py:36
  188.9 26.3 %gather_fusion = f32[256,2,8192]{2,1,0:T(2,128)} fusion(f32[2,128,8192]{2,0,1:T(2,128)} %get-tuple-element.301, s32[1024]{0:T(1024)S(1)} %pad_clamp_fusion.4), kind=kCustom, calls=%fused_computation.1.clone.clone.1 | custom fusion | bytes 33555456 | tf_op jit(solution)/shard_map/while/body/eval_jaxpr/jit(_take)/gather | solution.py:35
  215.1 13.0 %select_bitcast_fusion.2 = f32[2,16,16,8192]{3,0,2,1:T(2,128)} fusion(f32[16,16,2,8192]{3,2,1,0:T(2,128)} %bitcast.157, pred[16,16]{1,0:T(8,128)(4,1)S(1)} %compare_and_fusion.4), kind=kLoop, calls=%fused_computation.3.clone.1 | loop fusion | flops 4194304 | bytes 33554688 | tf_op jit(solution)/shard_map/while/body/eval_jaxpr/jit(_take)/select_n | solution.py:35
  228.1 21.0 %fusion.32 = (f32[1,16,16,8192]{3,0,2,1:T(1,128)S(1)}, f32[1,16,16,8192]{3,0,2,1:T(1,128)}) fusion(f32[2,16,16,8192]{3,0,2,1:T(2,128)} %select_bitcast_fusion.2), kind=kLoop, calls=%fused_computation.87.clone.1 | loop fusion | bytes 33554432 | tf_op jit(solution)/shard_map/while/body/eval_jaxpr/slice | solution.py:39
  249.2 24.0 %fusion.33 = (f32[16,8192]{1,0:T(8,128)S(1)}, f32[16,8192]{1,0:T(8,128)S(1)}) fusion(f32[1,16,16,8192]{3,0,2,1:T(1,128)} %get-tuple-element.268, f32[1,16,16,8192]{3,0,2,1:T(1,128)S(1)} %get-tuple-element.269, f32[16,16,2,8192]{3,1,0,2:T(8,128)} %copy_select_fusion.2, f32[16,16]{1,0:T(8,128)S(1)} %compare_convert_fusion.2), kind=kLoop, calls=%fused_computation.12.clone.1 | loop fusion | flops 20709376 | bytes 34604032 | tf_op jit(solution)/shard_map/while/body/eval_jaxpr/reduce_sum | solution.py:39
  274.0 29.8 %gather_fusion.1 = f32[256,2,8192]{2,1,0:T(2,128)} fusion(f32[316,2,8192]{2,1,0:T(2,128)} %get-tuple-element.298, s32[1024]{0:T(1024)S(1)} %pad_clamp_fusion.5), kind=kCustom, calls=%fused_computation.clone.clone.1 | custom fusion | bytes 33555456 | tf_op jit(solution)/shard_map/while/body/eval_jaxpr/jit(_take)/gather | solution.py:36
  303.8 18.0 %copy_select_fusion.2 = f32[16,16,2,8192]{3,1,0,2:T(8,128)} fusion(f32[16,16,2,8192]{3,2,1,0:T(2,128)} %bitcast.156, pred[16,16]{1,0:T(8,128)(4,1)S(1)} %compare_and_fusion.5), kind=kLoop, calls=%fused_computation.2.clone.1 | loop fusion | flops 4194304 | bytes 33554688 | tf_op jit(solution)/shard_map/while/body/eval_jaxpr/jit(_take)/select_n | solution.py:36
  321.7 26.3 %gather_fusion = f32[256,2,8192]{2,1,0:T(2,128)} fusion(f32[2,128,8192]{2,0,1:T(2,128)} %get-tuple-element.301, s32[1024]{0:T(1024)S(1)} %pad_clamp_fusion.4), kind=kCustom, calls=%fused_computation.1.clone.clone.1 | custom fusion | bytes 33555456 | tf_op jit(solution)/shard_map/while/body/eval_jaxpr/jit(_take)/gather | solution.py:35
  348.0 13.0 %select_bitcast_fusion.2 = f32[2,16,16,8192]{3,0,2,1:T(2,128)} fusion(f32[16,16,2,8192]{3,2,1,0:T(2,128)} %bitcast.157, pred[16,16]{1,0:T(8,128)(4,1)S(1)} %compare_and_fusion.4), kind=kLoop, calls=%fused_computation.3.clone.1 | loop fusion | flops 4194304 | bytes 33554688 | tf_op jit(solution)/shard_map/while/body/eval_jaxpr/jit(_take)/select_n | solution.py:35
  361.0 21.0 %fusion.32 = (f32[1,16,16,8192]{3,0,2,1:T(1,128)S(1)}, f32[1,16,16,8192]{3,0,2,1:T(1,128)}) fusion(f32[2,16,16,8192]{3,0,2,1:T(2,128)} %select_bitcast_fusion.2), kind=kLoop, calls=%fused_computation.87.clone.1 | loop fusion | bytes 33554432 | tf_op jit(solution)/shard_map/while/body/eval_jaxpr/slice | solution.py:39
  382.1 24.0 %fusion.33 = (f32[16,8192]{1,0:T(8,128)S(1)}, f32[16,8192]{1,0:T(8,128)S(1)}) fusion(f32[1,16,16,8192]{3,0,2,1:T(1,128)} %get-tuple-element.268, f32[1,16,16,8192]{3,0,2,1:T(1,128)S(1)} %get-tuple-element.269, f32[16,16,2,8192]{3,1,0,2:T(8,128)} %copy_select_fusion.2, f32[16,16]{1,0:T(8,128)S(1)} %compare_convert_fusion.2), kind=kLoop, calls=%fused_computation.12.clone.1 | loop fusion | flops 20709376 | bytes 34604032 | tf_op jit(solution)/shard_map/while/body/eval_jaxpr/reduce_sum | solution.py:39
  406.9 29.8 %gather_fusion.1 = f32[256,2,8192]{2,1,0:T(2,128)} fusion(f32[316,2,8192]{2,1,0:T(2,128)} %get-tuple-element.298, s32[1024]{0:T(1024)S(1)} %pad_clamp_fusion.5), kind=kCustom, calls=%fused_computation.clone.clone.1 | custom fusion | bytes 33555456 | tf_op jit(solution)/shard_map/while/body/eval_jaxpr/jit(_take)/gather | solution.py:36
  436.6 18.0 %copy_select_fusion.2 = f32[16,16,2,8192]{3,1,0,2:T(8,128)} fusion(f32[16,16,2,8192]{3,2,1,0:T(2,128)} %bitcast.156, pred[16,16]{1,0:T(8,128)(4,1)S(1)} %compare_and_fusion.5), kind=kLoop, calls=%fused_computation.2.clone.1 | loop fusion | flops 4194304 | bytes 33554688 | tf_op jit(solution)/shard_map/while/body/eval_jaxpr/jit(_take)/select_n | solution.py:36
  454.6 26.3 %gather_fusion = f32[256,2,8192]{2,1,0:T(2,128)} fusion(f32[2,128,8192]{2,0,1:T(2,128)} %get-tuple-element.301, s32[1024]{0:T(1024)S(1)} %pad_clamp_fusion.4), kind=kCustom, calls=%fused_computation.1.clone.clone.1 | custom fusion | bytes 33555456 | tf_op jit(solution)/shard_map/while/body/eval_jaxpr/jit(_take)/gather | solution.py:35
  480.9 13.0 %select_bitcast_fusion.2 = f32[2,16,16,8192]{3,0,2,1:T(2,128)} fusion(f32[16,16,2,8192]{3,2,1,0:T(2,128)} %bitcast.157, pred[16,16]{1,0:T(8,128)(4,1)S(1)} %compare_and_fusion.4), kind=kLoop, calls=%fused_computation.3.clone.1 | loop fusion | flops 4194304 | bytes 33554688 | tf_op jit(solution)/shard_map/while/body/eval_jaxpr/jit(_take)/select_n | solution.py:35
  493.9 21.0 %fusion.32 = (f32[1,16,16,8192]{3,0,2,1:T(1,128)S(1)}, f32[1,16,16,8192]{3,0,2,1:T(1,128)}) fusion(f32[2,16,16,8192]{3,0,2,1:T(2,128)} %select_bitcast_fusion.2), kind=kLoop, calls=%fused_computation.87.clone.1 | loop fusion | bytes 33554432 | tf_op jit(solution)/shard_map/while/body/eval_jaxpr/slice | solution.py:39
  514.9 24.0 %fusion.33 = (f32[16,8192]{1,0:T(8,128)S(1)}, f32[16,8192]{1,0:T(8,128)S(1)}) fusion(f32[1,16,16,8192]{3,0,2,1:T(1,128)} %get-tuple-element.268, f32[1,16,16,8192]{3,0,2,1:T(1,128)S(1)} %get-tuple-element.269, f32[16,16,2,8192]{3,1,0,2:T(8,128)} %copy_select_fusion.2, f32[16,16]{1,0:T(8,128)S(1)} %compare_convert_fusion.2), kind=kLoop, calls=%fused_computation.12.clone.1 | loop fusion | flops 20709376 | bytes 34604032 | tf_op jit(solution)/shard_map/while/body/eval_jaxpr/reduce_sum | solution.py:39
  539.7 29.8 %gather_fusion.1 = f32[256,2,8192]{2,1,0:T(2,128)} fusion(f32[316,2,8192]{2,1,0:T(2,128)} %get-tuple-element.298, s32[1024]{0:T(1024)S(1)} %pad_clamp_fusion.5), kind=kCustom, calls=%fused_computation.clone.clone.1 | custom fusion | bytes 33555456 | tf_op jit(solution)/shard_map/while/body/eval_jaxpr/jit(_take)/gather | solution.py:36
  569.5 18.0 %copy_select_fusion.2 = f32[16,16,2,8192]{3,1,0,2:T(8,128)} fusion(f32[16,16,2,8192]{3,2,1,0:T(2,128)} %bitcast.156, pred[16,16]{1,0:T(8,128)(4,1)S(1)} %compare_and_fusion.5), kind=kLoop, calls=%fused_computation.2.clone.1 | loop fusion | flops 4194304 | bytes 33554688 | tf_op jit(solution)/shard_map/while/body/eval_jaxpr/jit(_take)/select_n | solution.py:36
  587.5 26.3 %gather_fusion = f32[256,2,8192]{2,1,0:T(2,128)} fusion(f32[2,128,8192]{2,0,1:T(2,128)} %get-tuple-element.301, s32[1024]{0:T(1024)S(1)} %pad_clamp_fusion.4), kind=kCustom, calls=%fused_computation.1.clone.clone.1 | custom fusion | bytes 33555456 | tf_op jit(solution)/shard_map/while/body/eval_jaxpr/jit(_take)/gather | solution.py:35
  613.8 13.0 %select_bitcast_fusion.2 = f32[2,16,16,8192]{3,0,2,1:T(2,128)} fusion(f32[16,16,2,8192]{3,2,1,0:T(2,128)} %bitcast.157, pred[16,16]{1,0:T(8,128)(4,1)S(1)} %compare_and_fusion.4), kind=kLoop, calls=%fused_computation.3.clone.1 | loop fusion | flops 4194304 | bytes 33554688 | tf_op jit(solution)/shard_map/while/body/eval_jaxpr/jit(_take)/select_n | solution.py:35
  626.8 21.0 %fusion.32 = (f32[1,16,16,8192]{3,0,2,1:T(1,128)S(1)}, f32[1,16,16,8192]{3,0,2,1:T(1,128)}) fusion(f32[2,16,16,8192]{3,0,2,1:T(2,128)} %select_bitcast_fusion.2), kind=kLoop, calls=%fused_computation.87.clone.1 | loop fusion | bytes 33554432 | tf_op jit(solution)/shard_map/while/body/eval_jaxpr/slice | solution.py:39
  647.8 24.0 %fusion.33 = (f32[16,8192]{1,0:T(8,128)S(1)}, f32[16,8192]{1,0:T(8,128)S(1)}) fusion(f32[1,16,16,8192]{3,0,2,1:T(1,128)} %get-tuple-element.268, f32[1,16,16,8192]{3,0,2,1:T(1,128)S(1)} %get-tuple-element.269, f32[16,16,2,8192]{3,1,0,2:T(8,128)} %copy_select_fusion.2, f32[16,16]{1,0:T(8,128)S(1)} %compare_convert_fusion.2), kind=kLoop, calls=%fused_computation.12.clone.1 | loop fusion | flops 20709376 | bytes 34604032 | tf_op jit(solution)/shard_map/while/body/eval_jaxpr/reduce_sum | solution.py:39
  672.6 17.6 %slice.222 = f32[2,16,4096]{2,1,0:T(8,128)S(1)} slice(f32[2,16,8192]{2,1,0:T(8,128)S(1)} %get-tuple-element.158), slice={[0:2:1], [0:16:1], [1:8192:2]} | slice | bytes 1048576 | tf_op jit(solution)/shard_map/slice | solution.py:100
  690.2 17.8 %slice.219 = f32[2,16,4096]{2,1,0:T(8,128)S(1)} slice(f32[2,16,8192]{2,1,0:T(8,128)S(1)} %get-tuple-element.158), slice={[0:2:1], [0:16:1], [0:8192:2]} | slice | bytes 1048576 | tf_op jit(solution)/shard_map/slice | solution.py:99
  712.6 2.7 add_dynamic-update-slice_fusion.5
  715.3 2.8 add_dynamic-update-slice_fusion.4
  718.1 2.8 add_dynamic-update-slice_fusion.3
  723.6 2.7 add_dynamic-update-slice_fusion.1
  726.3 2.8 add_dynamic-update-slice_fusion
  733.0 3.4 collective-permute-start.2
  738.1 4.1 collective-permute-done.3
  743.4 15.4 %fusion.8 = f32[2,128,4096]{2,1,0:T(8,128)} fusion(f32[6,2,128,4096]{3,2,1,0:T(8,128)} %add_dynamic-update-slice_fusion, f32[6,2,128,3]{3,2,1,0:T(8,128)} %copy.53, f32[6,2,128,3]{3,2,1,0:T(8,128)S(1)} %copy.51, f32[2,128,4096]{2,1,0:T(8,128)} %param.11, f32[1,128,4096]{2,1,0:T(8,128)} %get-tuple-element.194, f32[1,128,4096]{2,1,0:T(8,128)S(1)} %get-tuple-element.192, ...), kind=kLoop, calls=%fused_computation.31 | loop fusion | flops 16777216 | bytes 42012672 | tf_op jit(solution)/shard_map/add | solution.py:112
  (164 shorter events, 27.0 us)
Async XLA Ops:
  7.2 133.3 %all-gather.2.cloned.1.call-start = ((), (), s32[]{:S(2)}) async-start(), calls=%async_computation | async-start | bytes 9437184 | tf_op jit(solution)/shard_map/all_gather | solution.py:93
  8.3 39.3 %collective-permute-start = (f32[2,128,3]{2,1,0:T(8,128)S(1)}, f32[2,128,3]{2,1,0:T(8,128)S(1)}, u32[]{:S(2)}, u32[]{:S(2)}) collective-permute-start(f32[2,128,3]{2,1,0:T(8,128)S(1)} %get-tuple-element.186), channel_id=1, source_target_pairs={{0,1},{1,2},{2,3},{3,0},{4,5},{5,6},{6,7},{7,4},{8,9},{9,10},{10,1... | collective-permute-start | bytes 9224 | tf_op jit(solution)/shard_map/ppermute | solution.py:16
  11.4 35.5 %collective-permute-start.1 = (f32[2,128,3]{2,1,0:T(8,128)S(1)}, f32[2,128,3]{2,1,0:T(8,128)S(1)}, u32[]{:S(2)}, u32[]{:S(2)}) collective-permute-start(f32[2,128,3]{2,1,0:T(8,128)S(1)} %get-tuple-element.187), channel_id=1, source_target_pairs={{1,0},{2,1},{3,2},{0,3},{5,4},{6,5},{7,6},{4,7},{9,8},{10,9},{11,1... | collective-permute-start | bytes 9224 | tf_op jit(solution)/shard_map/ppermute | solution.py:19
  22.1 25.5 %copy-start.10 = (f32[1,4096]{1,0:T(1,128)}, f32[1,4096]{1,0:T(1,128)S(1)}, u32[]{:S(2)}) copy-start(f32[1,4096]{1,0:T(1,128)S(1)} %get-tuple-element.212) | copy-start | bytes 49156
  22.2 25.4 %copy-start.14 = (f32[1,4096]{1,0:T(1,128)}, f32[1,4096]{1,0:T(1,128)S(1)}, u32[]{:S(2)}) copy-start(f32[1,4096]{1,0:T(1,128)S(1)} %get-tuple-element.209) | copy-start | bytes 49156
  22.2 25.4 %copy-start.16 = (f32[1,4096]{1,0:T(1,128)}, f32[1,4096]{1,0:T(1,128)S(1)}, u32[]{:S(2)}) copy-start(f32[1,4096]{1,0:T(1,128)S(1)} %get-tuple-element.210) | copy-start | bytes 49156
  22.2 25.4 %copy-start.18 = (f32[1,4096]{1,0:T(1,128)}, f32[1,4096]{1,0:T(1,128)S(1)}, u32[]{:S(2)}) copy-start(f32[1,4096]{1,0:T(1,128)S(1)} %get-tuple-element.211) | copy-start | bytes 49156
  22.2 25.4 %copy-start.24 = (f32[1,4096]{1,0:T(1,128)}, f32[1,4096]{1,0:T(1,128)S(1)}, u32[]{:S(2)}) copy-start(f32[1,4096]{1,0:T(1,128)S(1)} %get-tuple-element.213) | copy-start | bytes 49156
  22.2 25.4 %copy-start.26 = (f32[1,4096]{1,0:T(1,128)}, f32[1,4096]{1,0:T(1,128)S(1)}, u32[]{:S(2)}) copy-start(f32[1,4096]{1,0:T(1,128)S(1)} %get-tuple-element.208) | copy-start | bytes 49156
  22.3 41.6 %copy-start.12 = (f32[1,4096]{1,0:T(1,128)}, f32[1,4096]{1,0:T(1,128)S(1)}, u32[]{:S(2)}) copy-start(f32[1,4096]{1,0:T(1,128)S(1)} %get-tuple-element.206) | copy-start | bytes 49156
  22.3 41.6 %copy-start.20 = (f32[1,4096]{1,0:T(1,128)}, f32[1,4096]{1,0:T(1,128)S(1)}, u32[]{:S(2)}) copy-start(f32[1,4096]{1,0:T(1,128)S(1)} %get-tuple-element.203) | copy-start | bytes 49156
  22.3 41.6 %copy-start.22 = (f32[1,4096]{1,0:T(1,128)}, f32[1,4096]{1,0:T(1,128)S(1)}, u32[]{:S(2)}) copy-start(f32[1,4096]{1,0:T(1,128)S(1)} %get-tuple-element.204) | copy-start | bytes 49156
  22.3 41.6 %copy-start.28 = (f32[1,4096]{1,0:T(1,128)}, f32[1,4096]{1,0:T(1,128)S(1)}, u32[]{:S(2)}) copy-start(f32[1,4096]{1,0:T(1,128)S(1)} %get-tuple-element.205) | copy-start | bytes 49156
  22.3 41.6 %copy-start.30 = (f32[1,4096]{1,0:T(1,128)}, f32[1,4096]{1,0:T(1,128)S(1)}, u32[]{:S(2)}) copy-start(f32[1,4096]{1,0:T(1,128)S(1)} %get-tuple-element.207) | copy-start | bytes 49156
  22.3 41.6 %copy-start.32 = (f32[1,4096]{1,0:T(1,128)}, f32[1,4096]{1,0:T(1,128)S(1)}, u32[]{:S(2)}) copy-start(f32[1,4096]{1,0:T(1,128)S(1)} %get-tuple-element.202) | copy-start | bytes 49156
  33.3 29.0 %copy-start.2 = (f32[8,4096]{1,0:T(8,128)}, f32[8,4096]{1,0:T(8,128)S(1)}, u32[]{:S(2)}) copy-start(f32[8,4096]{1,0:T(8,128)S(1)} %slice.208) | copy-start | bytes 393220
  37.8 32.8 %copy-start.6 = (f32[8,4096]{1,0:T(8,128)}, f32[8,4096]{1,0:T(8,128)S(1)}, u32[]{:S(2)}) copy-start(f32[8,4096]{1,0:T(8,128)S(1)} %slice.190) | copy-start | bytes 393220
  42.3 20.0 %copy-start.4 = (f32[8,4096]{1,0:T(8,128)}, f32[8,4096]{1,0:T(8,128)S(1)}, u32[]{:S(2)}) copy-start(f32[8,4096]{1,0:T(8,128)S(1)} %slice.217) | copy-start | bytes 393220
  46.9 23.8 %copy-start.8 = (f32[8,4096]{1,0:T(8,128)}, f32[8,4096]{1,0:T(8,128)S(1)}, u32[]{:S(2)}) copy-start(f32[8,4096]{1,0:T(8,128)S(1)} %slice.206) | copy-start | bytes 393220
  47.6 16.3 %slice-start = ((s8[4325376]{0:T(1024)(128)(4,1)}), s8[4194304]{0:T(1024)(128)(4,1)S(1)}, s32[]{:S(2)}) async-start(s8[4325376]{0:T(1024)(128)(4,1)} %bitcast.158), calls=%async_computation.1 | async-start | bytes 8388608
  47.6 16.3 %slice-start.1 = ((s8[4325376]{0:T(1024)(128)(4,1)}), s8[131072]{0:T(1024)(128)(4,1)S(1)}, s32[]{:S(2)}) async-start(s8[4325376]{0:T(1024)(128)(4,1)} %bitcast.158), calls=%async_computation.2 | async-start | bytes 262144
  62.3 2.2 copy-start
  80.3 6.2 copy-start.36
  80.3 6.2 copy-start.34
  80.3 6.2 copy-start.35
  672.6 37.4 %copy-start.1 = (f32[2,16,8192]{2,1,0:T(8,128)}, f32[2,16,8192]{2,1,0:T(8,128)S(1)}, u32[]{:S(2)}) copy-start(f32[2,16,8192]{2,1,0:T(8,128)S(1)} %get-tuple-element.158) | copy-start | bytes 3145732
  672.6 35.5 %copy-start.7 = (f32[8,4096]{1,0:T(8,128)S(1)}, f32[8,4096]{1,0:T(8,128)}, u32[]{:S(2)}) copy-start(f32[8,4096]{1,0:T(8,128)} %copy-done.6) | copy-start | bytes 393220
  672.6 35.5 %copy-start.9 = (f32[8,4096]{1,0:T(8,128)S(1)}, f32[8,4096]{1,0:T(8,128)}, u32[]{:S(2)}) copy-start(f32[8,4096]{1,0:T(8,128)} %copy-done.8) | copy-start | bytes 393220
  708.0 1.9 copy-start.3
  708.0 1.9 copy-start.5
  709.9 2.6 copy-start.27
  709.9 2.6 copy-start.33
  712.6 2.7 copy-start.25
  712.6 2.7 copy-start.31
  715.3 2.8 copy-start.11
  715.3 2.8 copy-start.13
  718.1 2.8 copy-start.19
  718.1 2.8 copy-start.29
  720.9 2.7 copy-start.17
  720.9 2.7 copy-start.23
  723.6 2.7 copy-start.15
  723.6 2.7 copy-start.21
  733.0 4.8 collective-permute-start.2
  736.6 5.6 collective-permute-start.3
Sparse Core Ops, SparseCore 0:
  86.6 53.8 all-gather.1
where the time goes:
time: 775 us; the launch traced here: 766 us
  local copies, waits for them, and re-layouts  401 us (52%)
  other arithmetic  282 us (36%)
  waiting for transfers between devices  59.1 us (8%)
  between operations  14.8 us (2%)
  starting transfers between devices  8.62 us (1%)
    gather x4, local copies, waits for them, and re-layouts, advance(): coupling = jnp.take(table, operator_cols, axis=0)  119 us
    gather x4, local copies, waits for them, and re-layouts, advance(): source = jnp.take(pattern, partner_cols, axis=1)  105 us
    reduce_sum x4, other arithmetic, advance(): real_part = jnp.sum(coup_real * source[0] - coup_imag * source[1], axis=1)  96 us
    slice x4, local copies, waits for them, and re-layouts, advance(): real_part = jnp.sum(coup_real * source[0] - coup_imag * source[1], axis=1)  84.2 us
    select_n x8, other arithmetic, advance(): coupling = jnp.take(table, operator_cols, axis=0)  71.9 us
    all_gather x1, waiting for transfers between devices, local(): whole = lax.all_gather(parent, 'cluster', axis=1, tiled=True)  53.8 us
    select_n x8, other arithmetic, advance(): source = jnp.take(pattern, partner_cols, axis=1)  52 us
    slice x1, local copies, waits for them, and re-layouts, local(): shift_even = phase_spread(incoming[:, :, 0::2], cos_even, sin_even)  17.8 us
  transfers between devices with their start and end apart: 5, of which 3 were waited for; matrix products, arithmetic and copies ran while one was open for 5% of the time, Pallas kernels for 0%

commit v1 on v0

--- a/solution.py
+++ b/solution.py
@@ -1,18 +1,404 @@
+import functools
+
 import jax
 import jax.numpy as jnp
 from jax import lax
+from jax.experimental import pallas as pl
+from jax.experimental.pallas import tpu as pltpu
 from jax.sharding import PartitionSpec as P
 
 TAPS = 6
 CHILDREN = 8
+LANES = 128
+RIM = TAPS // 2
+GROUP = 4
+
+
+def split(values):
+    high = values.astype(jnp.bfloat16)
+    low = (values - high.astype(jnp.float32)).astype(jnp.bfloat16)
+    return high, low
+
+
+def band(weight):
+    rows = lax.broadcasted_iota(jnp.int32, (LANES, 2 * LANES), 0)
+    half = lax.broadcasted_iota(jnp.int32, (LANES, 2 * LANES), 1) // 2
+    tap = rows - half + (RIM - 1)
+    main = jnp.zeros((LANES, 2 * LANES), jnp.float32)
+    for w in range(TAPS):
+        main = jnp.where(tap == w, weight[w : w + 1, :], main)
+    after = tap + LANES
+    before = tap - LANES
+    rim = jnp.zeros((LANES, 2 * LANES), jnp.float32)
+    for w in range(TAPS):
+        hit = jnp.where(rows < LANES // 2, after, before) == w
+        rim = jnp.where(hit, weight[w : w + 1, :], rim)
+    return jnp.concatenate([main, rim], axis=0)
+
+
+def merge(first, second, step, sub):
+    low = (sub & step) == 0
+    return jnp.where(low, first, second) + pltpu.roll(jnp.where(low, second, first), step, 0)
+
+
+def sublane_sums(blocks, sub):
+    for step in (1, 2, 4):
+        blocks = [merge(blocks[i], blocks[i + 1], step, sub) for i in range(0, len(blocks), 2)]
+    return blocks[0]
+
+
+def aggregate_kernel(base, me_ref, x_ref, left_ref, right_ref, edge_ref, w_ref, c_ref, s_ref, *rest):
+    outs, (up_ref,) = rest[:-1], rest[-1:]
+    step = pl.program_id(0)
+    slices = pl.num_programs(0)
+    piece = me_ref[0] ^ (base + step)
+    last = me_ref[1] - 1
+    blocks = x_ref.shape[2] // LANES
+    rows = x_ref.shape[0] * x_ref.shape[1]
+    parents = x_ref.shape[1] // CHILDREN
+    lane = lax.broadcasted_iota(jnp.int32, (rows, LANES), 1)
+    sub = lax.broadcasted_iota(jnp.int32, (8, LANES), 0)
+    edge = edge_ref[...].reshape(rows, LANES)
+    left = jnp.where(piece == 0, edge, left_ref[...].reshape(rows, LANES))
+    right = jnp.where(piece == last, edge, right_ref[...].reshape(rows, LANES))
+    parts = [x_ref[:, :, b * LANES : (b + 1) * LANES].reshape(rows, LANES) for b in range(blocks)]
+    parts = [split(part) for part in [left] + parts + [right]]
+    for b in range(blocks):
+        columns = slice(2 * LANES * b, 2 * LANES * (b + 1))
+        high, low = split(band(w_ref[:, columns]))
+        here, before, after = parts[b + 1], parts[b], parts[b + 2]
+        rim = [jnp.where(lane < LANES // 2, after[i], before[i]) for i in range(2)]
+        left_hand = jnp.concatenate([here[0], rim[0], here[1], rim[1], here[0], rim[0]], axis=1)
+        right_hand = jnp.concatenate([high, high, low], axis=0)
+        up_ref[:, columns] = jnp.dot(left_hand, right_hand, preferred_element_type=jnp.float32)
+
+    for i in range(len(outs)):
+
+        @pl.when(step == i)
+        def _(out_ref=outs[i]):
+            for quad in range(blocks // 2):
+
+                def one(p, carry):
+                    gathered = []
+                    for b in range(4):
+                        col = slice(LANES * (4 * quad + b), LANES * (4 * quad + b + 1))
+                        cosine, sine = c_ref[:, col], s_ref[:, col]
+                        real = up_ref[pl.ds(p * CHILDREN, CHILDREN), col]
+                        imag = up_ref[pl.ds((parents + p) * CHILDREN, CHILDREN), col]
+                        gathered.append(cosine * real - sine * imag)
+                        gathered.append(cosine * imag + sine * real)
+                    out_ref[p, 8 * quad : 8 * quad + 8, :] = sublane_sums(gathered, sub)
+                    return carry
+
+                lax.fori_loop(0, parents, one, 0, unroll=2)
+
+
+def aggregate(me, total, base, count, child, edge, weight, cosine, sine):
+    comps, children, width = child.shape
+    span = width // total
+    blocks = span // LANES
+    parents = children // CHILDREN
+    where = jnp.stack([me, jnp.int32(total)])
+    grid_spec = pltpu.PrefetchScalarGridSpec(
+        num_scalar_prefetch=1,
+        grid=(count,),
+        in_specs=[
+            pl.BlockSpec((comps, children, span), lambda g, m: (0, 0, m[0] ^ (base + g))),
+            pl.BlockSpec(
+                (comps, children, LANES),
+                lambda g, m: (0, 0, jnp.maximum((m[0] ^ (base + g)) * blocks - 1, 0)),
+            ),
+            pl.BlockSpec(
+                (comps, children, LANES),
+                lambda g, m: (0, 0, jnp.minimum(((m[0] ^ (base + g)) + 1) * blocks, total * blocks - 1)),
+            ),
+            pl.BlockSpec((comps, children, LANES), lambda g, m: (0, 0, 0)),
+            pl.BlockSpec((TAPS, 2 * span), lambda g, m: (0, m[0] ^ (base + g))),
+            pl.BlockSpec((CHILDREN, 2 * span), lambda g, m: (0, m[0] ^ (base + g))),
+            pl.BlockSpec((CHILDREN, 2 * span), lambda g, m: (0, m[0] ^ (base + g))),
+        ],
+        out_specs=[pl.BlockSpec((parents, 4 * blocks, LANES), lambda g, m: (0, 0, 0))] * count,
+        scratch_shapes=[pltpu.VMEM((comps * children, 2 * span), jnp.float32)],
+    )
+    return pl.pallas_call(
+        functools.partial(aggregate_kernel, base),
+        grid_spec=grid_spec,
+        out_shape=[jax.ShapeDtypeStruct((parents, 4 * blocks, LANES), jnp.float32)] * count,
+        name="aggregate",
+        cost_estimate=pl.CostEstimate(flops=4 << 30, bytes_accessed=6 << 20, transcendentals=0),
+    )(where, child, child, child, edge, weight, cosine, sine)
+
+
+def translate_kernel(base, count, me_ref, partner_ref, op_ref, len_ref, table_ref, *rest):
+    total = me_ref.shape[0]
+    sources, outs = rest[:total], rest[total : total + count]
+    held, swapped = rest[total + count :]
+    parents, rows, _ = sources[0].shape
+    me = me_ref[0]
+    odd = (lax.broadcasted_iota(jnp.int32, (rows, LANES), 0) & 1) == 1
+    for k in range(total):
+        first = (me ^ k) * parents
+
+        def place(p, carry, k=k, first=first):
+            block = sources[k][p]
+            held[first + p] = block
+            swapped[first + p] = jnp.where(odd, pltpu.roll(block, 1, 0), pltpu.roll(block, rows - 1, 0))
+            return carry
+
+        lax.fori_loop(0, parents, place, 0, unroll=4)
+
+    for i in range(count):
+        first = (me ^ (base + i)) * parents
+
+        def receive(q, carry, out_ref=outs[i], first=first):
+            row = first + q
+
+            def add(step, totals):
+                direct, crossed = totals
+                for u in range(GROUP):
+                    slot = step * GROUP + u
+                    operator = table_ref[op_ref[row, slot]]
+                    partner = partner_ref[row, slot]
+                    direct = direct + operator * held[partner]
+                    crossed = crossed + operator * swapped[partner]
+                return direct, crossed
+
+            zero = jnp.zeros((rows, LANES), jnp.float32)
+            direct, crossed = lax.fori_loop(0, (len_ref[row] + GROUP - 1) // GROUP, add, (zero, zero))
+            real = direct - pltpu.roll(direct, rows - 1, 0)
+            imag = crossed + pltpu.roll(crossed, 1, 0)
+            out_ref[q] = jnp.where(odd, imag, real)
+            return carry
+
+        lax.fori_loop(0, parents, receive, 0)
+
+
+def translate(me, base, count, partners, operators, lengths, table, sources):
+    total = len(sources)
+    parents, rows, lanes = sources[0].shape
+    smem = pl.BlockSpec(memory_space=pltpu.SMEM)
+    vmem = pl.BlockSpec(memory_space=pltpu.VMEM)
+    return pl.pallas_call(
+        functools.partial(translate_kernel, base, count),
+        in_specs=[smem] * 4 + [vmem] * (1 + total),
+        out_specs=[vmem] * count,
+        out_shape=[jax.ShapeDtypeStruct((parents, rows, lanes), jnp.float32)] * count,
+        scratch_shapes=[pltpu.VMEM((total * parents, rows, lanes), jnp.float32)] * 2,
+        name="translate",
+        cost_estimate=pl.CostEstimate(flops=4 << 30, bytes_accessed=4 << 20, transcendentals=0),
+    )(jnp.full((total,), me, jnp.int32), partners, operators, lengths, table, *sources)
+
+
+def spread_kernel(me_ref, local_ref, w_ref, wn_ref, c_ref, cn_ref, s_ref, sn_ref, *rest):
+    total = me_ref.shape[0]
+    sources = rest[:total]
+    incoming_ref, out_ref, first_ref, last_ref = rest[total : total + 4]
+    fields, shifted, carried, trailing = rest[total + 4 :]
+    parents, rows_of, _ = sources[0].shape
+    blocks = rows_of // 4
+    comps, children, _ = out_ref.shape
+    rows = comps * children
+    step = pl.program_id(0)
+    me = me_ref[0]
+    lane = lax.broadcasted_iota(jnp.int32, (rows, LANES), 1)
+
+    @pl.when(step == 0)
+    def _():
+        for k in range(total):
+            fields[me ^ k] = sources[k][...].reshape(parents * rows_of, LANES)
+
+    for b in range(2 * blocks):
+        for comp in range(comps):
+            for half in range(parents // 8):
+                incoming_ref[comp, 8 * half : 8 * half + 8, b * LANES : (b + 1) * LANES] = fields[
+                    step, pl.ds(8 * half * rows_of + 2 * b + comp, 8, stride=rows_of), :
+                ]
+
+    def block(piece, index, weight, cos_ref, sin_ref):
+        for half in range(2):
+            b = 2 * index + half
+            columns = slice(LANES * b, LANES * (b + 1))
+            cosine, sine = cos_ref[:, columns], sin_ref[:, columns]
+
+            def one(p, carry):
+                at = p * rows_of + 2 * b
+                real = jnp.broadcast_to(fields[piece, pl.ds(at, 1), :], (CHILDREN, LANES))
+                imag = jnp.broadcast_to(fields[piece, pl.ds(at + 1, 1), :], (CHILDREN, LANES))
+                into = slice(half * LANES, (half + 1) * LANES)
+                shifted[pl.ds(p * CHILDREN, CHILDREN), into] = cosine * real + sine * imag
+                shifted[pl.ds((parents + p) * CHILDREN, CHILDREN), into] = cosine * imag - sine * real
+                return carry
+
+            lax.fori_loop(0, parents, one, 0, unroll=4)
+        high, low = split(shifted[...])
+        whigh, wlow = split(band(weight))
+        left_hand = jnp.concatenate([high, low, high], axis=1)
+        right_hand = jnp.concatenate([whigh, whigh, wlow], axis=1)
+        both = lax.dot_general(
+            left_hand, right_hand, (((1,), (1,)), ((), ())), preferred_element_type=jnp.float32
+        )
+        return both[:, :LANES], both[:, LANES:]
+
+    @pl.when(step == 0)
+    def _():
+        main, rim = block(0, 0, w_ref[:, : 2 * LANES], c_ref, s_ref)
+        carried[0] = main
+        carried[1] = rim
+        trailing[...] = jnp.zeros((rows, LANES), jnp.float32)
+        first_ref[...] = rim.reshape(comps, children, LANES)
+
+    def finish(index, main, before, after):
+        columns = slice(LANES * index, LANES * (index + 1))
+        value = main + jnp.where(lane < LANES // 2, before, after)
+        out_ref[:, :, columns] = local_ref[:, :, columns] + value.reshape(comps, children, LANES)
+
+    for b in range(1, blocks):
+        main, rim = block(step, b, w_ref[:, 2 * LANES * b : 2 * LANES * (b + 1)], c_ref, s_ref)
+        finish(b - 1, carried[0], trailing[...], rim)
+        trailing[...] = carried[1]
+        carried[0] = main
+        carried[1] = rim
+
+    @pl.when(step < total - 1)
+    def _():
+        main, rim = block(step + 1, 0, wn_ref[...], cn_ref, sn_ref)
+        finish(blocks - 1, carried[0], trailing[...], rim)
+        trailing[...] = carried[1]
+        carried[0] = main
+        carried[1] = rim
+
+    @pl.when(step == total - 1)
+    def _():
+        finish(blocks - 1, carried[0], trailing[...], jnp.zeros((rows, LANES), jnp.float32))
+        last_ref[...] = carried[1].reshape(comps, children, LANES)
+
+
+def spread(me, child_local, weight, cosine, sine, sources):
+    total = len(sources)
+    parents, rows_of, _ = sources[0].shape
+    comps, children, width = child_local.shape
+    span = width // total
+    blocks = span // LANES
+    smem = pl.BlockSpec(memory_space=pltpu.SMEM)
+    held = pl.BlockSpec((parents, rows_of, LANES), lambda g: (0, 0, 0))
+    edge = pl.BlockSpec((comps, children, LANES), lambda g: (0, 0, 0))
+
+    def after(g):
+        return (0, jnp.minimum((g + 1) * blocks, total * blocks - 1))
+
+    return pl.pallas_call(
+        spread_kernel,
+        grid=(total,),
+        in_specs=[
+            smem,
+            pl.BlockSpec((comps, children, span), lambda g: (0, 0, g)),
+            pl.BlockSpec((TAPS, 2 * span), lambda g: (0, g)),
+            pl.BlockSpec((TAPS, 2 * LANES), after),
+            pl.BlockSpec((CHILDREN, 2 * span), lambda g: (0, g)),
+            pl.BlockSpec((CHILDREN, 2 * LANES), after),
+            pl.BlockSpec((CHILDREN, 2 * span), lambda g: (0, g)),
+            pl.BlockSpec((CHILDREN, 2 * LANES), after),
+        ]
+        + [held] * total,
+        out_specs=[
+            pl.BlockSpec((comps, parents, 2 * span), lambda g: (0, 0, g)),
+            pl.BlockSpec((comps, children, span), lambda g: (0, 0, g)),
+            edge,
+            edge,
+        ],
+        out_shape=[
+            jax.ShapeDtypeStruct((comps, parents, 2 * width), jnp.float32),
+            jax.ShapeDtypeStruct((comps, children, width), jnp.float32),
+            jax.ShapeDtypeStruct((comps, children, LANES), jnp.float32),
+            jax.ShapeDtypeStruct((comps, children, LANES), jnp.float32),
+        ],
+        scratch_shapes=[
+            pltpu.VMEM((total, parents * rows_of, LANES), jnp.float32),
+            pltpu.VMEM((comps * children, 2 * LANES), jnp.float32),
+            pltpu.VMEM((2, comps * children, LANES), jnp.float32),
+            pltpu.VMEM((comps * children, LANES), jnp.float32),
+        ],
+        name="spread",
+        cost_estimate=pl.CostEstimate(flops=8 << 30, bytes_accessed=12 << 20, transcendentals=0),
+    )(
+        jnp.full((total,), me, jnp.int32),
+        child_local,
+        weight,
+        weight,
+        cosine,
+        cosine,
+        sine,
+        sine,
+        *sources,
+    )
+
+
+def ring(count):
+    forward = [(i, (i + 1) % count) for i in range(count)]
+    return forward, [(target, source) for source, target in forward]
+
+
+def fast(
+    child_pattern,
+    child_local,
+    interp_weight,
+    child_phase,
+    translator,
+    partners,
+    operator_id,
+    list_len,
+):
+    total = lax.axis_size("cluster")
+    me = lax.axis_index("cluster")
+    comps, children, width = child_pattern.shape
+    forward, backward = ring(lax.axis_size("sample"))
+    low = lax.ppermute(child_pattern[:, :, width - (RIM - 1) :], "sample", forward)
+    high = lax.ppermute(child_pattern[:, :, :RIM], "sample", backward)
+    gap = jnp.zeros((comps, children, LANES - TAPS + 1), jnp.float32)
+    edge = jnp.concatenate([high, gap, low], axis=2)
+    cosine = jnp.cos(child_phase)
+    sine = jnp.sin(child_phase)
+
+    def swap(block, k):
+        if k == 0:
+            return block
+        return lax.ppermute(block, "cluster", [(i, i ^ k) for i in range(total)])
+
+    half = total // 2
+    sent = [None] * total
+    for base in (half, 0):
+        made = aggregate(me, total, base, half, child_pattern, edge, interp_weight, cosine, sine)
+        for i in range(half):
+            sent[base + i] = made[i]
+    sources = [swap(sent[k], k) for k in range(total)]
+
+    count, _, samples = translator.shape
+    table = translator.reshape(count, comps, samples // LANES, LANES).transpose(0, 2, 1, 3)
+    table = table.reshape(count, 2 * samples // LANES, LANES)
+    rows = 2 * samples // LANES // total
+    table = lax.dynamic_slice_in_dim(table, me * rows, rows, 1)
+    table = jnp.pad(table, ((0, 1), (0, 0), (0, 0)))
+    alive = jnp.arange(operator_id.shape[1])[None, :] < list_len[:, None]
+    operators = jnp.where(alive, operator_id, count)
+    back = [None] * total
+    for base in (half, 0):
+        made = translate(me, base, half, partners, operators, list_len, table, sources)
+        for i in range(half):
+            back[base + i] = made[i]
+    fields = [swap(back[k], k) for k in range(total)]
+    incoming, child_incoming, first, last = spread(
+        me, child_local, interp_weight, cosine, sine, fields
+    )
+    low = lax.ppermute(last[:, :, :RIM], "sample", forward)
+    high = lax.ppermute(first[:, :, LANES - RIM + 1 :], "sample", backward)
+    child_incoming = child_incoming.at[:, :, :RIM].add(low)
+    child_incoming = child_incoming.at[:, :, width - RIM + 1 :].add(high)
+    return incoming, child_incoming
 
 
 def with_halo(block, sides, width):
     for axis, dim in sides:
-        count = lax.axis_size(axis)
-        forward = [(i, i + 1) for i in range(count - 1)]
-        forward.append((count - 1, 0))
-        backward = [(target, source) for source, target in forward]
+        forward, backward = ring(lax.axis_size(axis))
         low = lax.ppermute(
             lax.slice_in_dim(block, block.shape[dim] - width, None, axis=dim), axis, forward
         )
@@ -21,7 +407,7 @@
     return block
 
 
-def translate(pattern, table, partner_rows, operator_rows, lengths):
+def translate_rows(pattern, table, partner_rows, operator_rows, lengths):
     receivers = partner_rows.shape[0]
     slot_count = partner_rows.shape[1]
     group_size = 16
@@ -57,7 +443,7 @@
     return jnp.stack([shifted_real, shifted_imag]).reshape(2, -1, incoming.shape[2])
 
 
-def local(
+def plain(
     child_pattern,
     child_local,
     interp_weight,
@@ -95,7 +481,7 @@
     own_partners = lax.dynamic_slice_in_dim(partners, first_row, parent_count, 0)
     own_operators = lax.dynamic_slice_in_dim(operator_id, first_row, parent_count, 0)
     own_lengths = lax.dynamic_slice_in_dim(list_len, first_row, parent_count, 0)
-    incoming = translate(whole, translator, own_partners, own_operators, own_lengths)
+    incoming = translate_rows(whole, translator, own_partners, own_operators, own_lengths)
     shift_even = phase_spread(incoming[:, :, 0::2], cos_even, sin_even)
     shift_odd = phase_spread(incoming[:, :, 1::2], cos_odd, sin_odd)
     weighted = jnp.stack(
@@ -111,6 +497,14 @@
         offset = 2 * rim_width - 1 - tap
         child_incoming = child_incoming + padded_weighted[tap, :, :, offset : offset + half_samples]
     return (incoming, child_incoming)
+
+
+def local(child_pattern, *rest):
+    total = lax.axis_size("cluster")
+    share = child_pattern.shape[2] // total
+    fits = total & (total - 1) == 0 and share >= 2 * LANES and share % (2 * LANES) == 0
+    fits = fits and share * total == child_pattern.shape[2]
+    return (fast if fits else plain)(child_pattern, *rest)
 
 
 def solution(mesh):

time: 775 us -> 130 us (0.17); the launches traced: 766 us -> 129 us
  local copies, waits for them, and re-layouts: 401 us -> 14.7 us
  other arithmetic: 282 us -> 4.06 us
  Pallas kernels: 0 us -> 67.8 us
  waiting for transfers between devices: 59.1 us -> 19.7 us
  between operations: 14.8 us -> 0.84 us
  starting transfers between devices: 8.62 us -> 21.5 us
    gather x8 -> x0, local copies, waits for them, and re-layouts: 224 us -> none  [the longest x4 119 us: advance(): coupling = jnp.take(table, operator_cols, axis=0)]
    slice x18 -> x3, local copies, waits for them, and re-layouts: 151 us -> 2.91 us  [the longest x1 0.99 us: fast(): high = lax.ppermute(first[:, :, LANES - RIM + 1:], 'sample', backward)]
    select_n x16 -> x1, other arithmetic: 124 us -> 0.71 us  [fast(): operators = jnp.where(alive, operator_id, count)]
    reduce_sum x6 -> x0, other arithmetic: 99 us -> none  [the longest x4 96 us: advance(): real_part = jnp.sum(coup_real * source[0] - coup_imag * source[1], axis=1)]
    pallas_call x0 -> x5, Pallas kernels: none -> 67.8 us  [the longest x2 30.6 us: translate(): pl.pallas_call(functools.partial(translate_kernel, base, count), in_specs...]
    all_gather x1 -> x0, waiting for transfers between devices: 53.8 us -> none  [local(): whole = lax.all_gather(parent, 'cluster', axis=1, tiled=True)]
    add x13 -> x2, other arithmetic: 41.9 us -> 1.93 us  [the longest x1 1 us: fast(): child_incoming = child_incoming.at[:, :, width - RIM + 1:].add(high)]
    ppermute x4 -> x18, waiting for transfers between devices: 5.25 us -> 19.7 us  [the longest x14 16.2 us: swap(): return lax.ppermute(block, 'cluster', [(i, i ^ k) for i in range(total)])]
  transfers between devices with their start and end apart: 5 -> 18, of which waited for: 3 -> 7; matrix products, arithmetic and copies ran while one was open for 5% -> 10% of each run, Pallas kernels for 0% -> 16%
where the time goes in v1:
time: 130 us; the launch traced here: 129 us
  Pallas kernels  67.8 us (52%)
  starting transfers between devices  21.5 us (17%)
  waiting for transfers between devices  19.7 us (15%)
  local copies, waits for them, and re-layouts  14.7 us (11%)
  other arithmetic  4.06 us (3%)
    pallas_call x2, Pallas kernels, translate(): pl.pallas_call(functools.partial(translate_kernel, base, count), in_specs...  30.6 us
    pallas_call x1, Pallas kernels, spread(): pl.pallas_call(spread_kernel, grid=(total,), in_specs=[smem, pl.BlockSpec...  20.4 us
    pallas_call x2, Pallas kernels, aggregate(): pl.pallas_call(functools.partial(aggregate_kernel, base), grid_spec=grid_...  16.8 us
    ppermute x14, waiting for transfers between devices, swap(): return lax.ppermute(block, 'cluster', [(i, i ^ k) for i in range(total)])  16.2 us
    ppermute x14, starting transfers between devices, swap(): return lax.ppermute(block, 'cluster', [(i, i ^ k) for i in range(total)])  12.4 us
    ppermute x1, starting transfers between devices, fast(): high = lax.ppermute(child_pattern[:, :, :RIM], 'sample', backward)  5.13 us
    ppermute x1, starting transfers between devices, fast(): high = lax.ppermute(first[:, :, LANES - RIM + 1:], 'sample', backward)  3.86 us
    ppermute x1, waiting for transfers between devices, fast(): low = lax.ppermute(last[:, :, :RIM], 'sample', forward)  3.52 us
  transfers between devices with their start and end apart: 18, of which 7 were waited for; matrix products, arithmetic and copies ran while one was open for 10% of the time, Pallas kernels for 16%

profile of v1, /device:TPU:0, one launch (start us, length us, event | category | flops | bytes accessed | tf_op | source)
XLA Modules:
  0.0 128.7 jit_solution(11752037318156370475)
XLA Ops:
  0.6 0.9 slice.60
  1.6 5.1 %collective-permute-start = (f32[2,128,3]{2,1,0:T(8,128)S(1)}, f32[2,128,3]{2,1,0:T(8,128)S(1)}, u32[]{:S(2)}, u32[]{:S(2)}) collective-permute-start(f32[2,128,3]{2,1,0:T(8,128)S(1)} %slice.60), channel_id=1, source_target_pairs={{1,0},{2,1},{3,2},{0,3},{5,4},{6,5},{7,6},{4,7},{9,8},{10,9},{11,1... | collective-permute-start | bytes 9224 | tf_op jit(solution)/shard_map/ppermute | solution.py:356
  6.7 1.0 slice.61
  7.7 0.1 collective-permute-start.1
  7.8 2.6 %fusion.1 = (f32[8,8192]{1,0:T(8,128)}, f32[8,8192]{1,0:T(8,128)}) fusion(f32[8,8192]{1,0:T(8,128)} %param.15), kind=kLoop, calls=%fused_computation.7 | loop fusion | bytes 786432 | tf_op jit(solution)/shard_map/sin | solution.py:360
  10.3 1.9 %constant_dynamic-slice_fusion = f32[316,16,128]{2,1,0:T(8,128)S(1)} fusion(f32[316,128,128]{2,1,0:T(8,128)} %bitcast.7, s32[]{:T(128)S(6)} %select_n.8), kind=kLoop, calls=%fused_computation.6 | loop fusion | bytes 5177348 | tf_op jit(solution)/shard_map/dynamic_slice | solution.py:379
  12.3 0.7 pad_add_fusion.me_ref
  12.9 0.7 copy.12.partner_ref
  13.7 0.1 copy.10
  13.7 1.7 %pad.8.table_ref = f32[317,16,128]{2,1,0:T(8,128)} pad(f32[316,16,128]{2,1,0:T(8,128)S(1)} %constant_dynamic-slice_fusion, f32[]{:T(128)} %constant.70.clone.1), padding=0_1x0_0x0_0 | pad | bytes 5185540 | tf_op jit(solution)/shard_map/jit(_pad)/pad | solution.py:380
  15.4 0.1 pad.10.clone
  15.5 0.8 pad_maximum_fusion.edge_ref
  16.3 8.3 %aggregate.3 = (f32[16,16,128]{2,1,0:T(8,128)}, f32[16,16,128]{2,1,0:T(8,128)}, f32[16,16,128]{2,1,0:T(8,128)}, f32[16,16,128]{2,1,0:T(8,128)}) custom-call(s32[2]{0:T(128)} %pad_add_fusion.me_ref, f32[2,128,4096]{2,1,0:T(8,128)} %right_ref.3, f32[2,128,4096]{2,1,0:T(8,128)} %right_ref.3, f32[2,128,4096]{2,1,0:T(8,128)} %right_ref.3, ...), custom_call_target="tpu_custom_call" | custom-call | flops 4294967296 | bytes 6291456 | tf_op jit(solution)/shard_map/aggregate/pallas_call | solution.py:123
  24.6 1.5 %collective-permute-start.5 = (f32[16,16,128]{2,1,0:T(8,128)}, f32[16,16,128]{2,1,0:T(8,128)S(1)}, u32[]{:S(2)}, u32[]{:S(2)}) collective-permute-start(f32[16,16,128]{2,1,0:T(8,128)} %get-tuple-element.50), channel_id=1, source_target_pairs={{0,16},{4,20},{8,24},{12,28},{16,0},{20,4},{24,8},{28,12},{1,17},{... | collective-permute-start | bytes 393224 | tf_op jit(solution)/shard_map/ppermute | solution.py:365
  26.1 8.5 %aggregate.2 = (f32[16,16,128]{2,1,0:T(8,128)}, f32[16,16,128]{2,1,0:T(8,128)}, f32[16,16,128]{2,1,0:T(8,128)}, f32[16,16,128]{2,1,0:T(8,128)}) custom-call(s32[2]{0:T(128)} %pad_add_fusion.me_ref, f32[2,128,4096]{2,1,0:T(8,128)} %right_ref.3, f32[2,128,4096]{2,1,0:T(8,128)} %right_ref.3, f32[2,128,4096]{2,1,0:T(8,128)} %right_ref.3, ...), custom_call_target="tpu_custom_call" | custom-call | flops 4294967296 | bytes 6291456 | tf_op jit(solution)/shard_map/aggregate/pallas_call | solution.py:123
  34.6 1.7 %collective-permute-start.7 = (f32[16,16,128]{2,1,0:T(8,128)S(1)}, f32[16,16,128]{2,1,0:T(8,128)S(1)}, u32[]{:S(2)}, u32[]{:S(2)}) collective-permute-start(f32[16,16,128]{2,1,0:T(8,128)S(1)} %copy-done.16), channel_id=1, source_target_pairs={{0,24},{4,28},{8,16},{12,20},{16,8},{20,12},{24,0},{28,4},{1,25},{... | collective-permute-start | bytes 393224 | tf_op jit(solution)/shard_map/ppermute | solution.py:365
  36.4 1.0 collective-permute-start.8
  37.4 0.3 collective-permute-start.2
  37.7 1.5 %collective-permute-start.3 = (f32[16,16,128]{2,1,0:T(8,128)}, f32[16,16,128]{2,1,0:T(8,128)S(1)}, u32[]{:S(2)}, u32[]{:S(2)}) collective-permute-start(f32[16,16,128]{2,1,0:T(8,128)} %get-tuple-element.48), channel_id=1, source_target_pairs={{0,8},{4,12},{8,0},{12,4},{16,24},{20,28},{24,16},{28,20},{1,9},{5... | collective-permute-start | bytes 393224 | tf_op jit(solution)/shard_map/ppermute | solution.py:365
  39.2 0.0 collective-permute-start.4
  39.3 0.7 fusion.op_ref
  40.0 2.0 %collective-permute-done.7.rest_6_ = f32[16,16,128]{2,1,0:T(8,128)S(1)} collective-permute-done((f32[16,16,128]{2,1,0:T(8,128)S(1)}, f32[16,16,128]{2,1,0:T(8,128)S(1)}, u32[]{:S(2)}, u32[]{:S(2)}) %collective-permute-start.7) | collective-permute-done | bytes 131104 | tf_op jit(solution)/shard_map/ppermute | solution.py:365
  42.0 1.8 %collective-permute-done.8.rest_7_ = f32[16,16,128]{2,1,0:T(8,128)S(1)} collective-permute-done((f32[16,16,128]{2,1,0:T(8,128)S(1)}, f32[16,16,128]{2,1,0:T(8,128)S(1)}, u32[]{:S(2)}, u32[]{:S(2)}) %collective-permute-start.8) | collective-permute-done | bytes 131104 | tf_op jit(solution)/shard_map/ppermute | solution.py:365
  43.8 0.0 collective-permute-done.2.rest_1_
  43.8 2.8 %collective-permute-done.3.rest_2_ = f32[16,16,128]{2,1,0:T(8,128)S(1)} collective-permute-done((f32[16,16,128]{2,1,0:T(8,128)}, f32[16,16,128]{2,1,0:T(8,128)S(1)}, u32[]{:S(2)}, u32[]{:S(2)}) %collective-permute-start.3) | collective-permute-done | bytes 131104 | tf_op jit(solution)/shard_map/ppermute | solution.py:365
  46.6 3.1 %collective-permute-done.4.rest_3_ = f32[16,16,128]{2,1,0:T(8,128)S(1)} collective-permute-done((f32[16,16,128]{2,1,0:T(8,128)}, f32[16,16,128]{2,1,0:T(8,128)S(1)}, u32[]{:S(2)}, u32[]{:S(2)}) %collective-permute-start.4) | collective-permute-done | bytes 131104 | tf_op jit(solution)/shard_map/ppermute | solution.py:365
  49.7 0.5 broadcast_in_dim.14.me_ref
  50.2 0.1 copy-done.13
  50.3 18.2 %translate.3 = (f32[16,16,128]{2,1,0:T(8,128)}, f32[16,16,128]{2,1,0:T(8,128)}, f32[16,16,128]{2,1,0:T(8,128)}, f32[16,16,128]{2,1,0:T(8,128)}) custom-call(s32[8]{0:T(128)} %broadcast_in_dim.14.me_ref, s32[128,64]{1,0:T(8,128)} %copy.12.partner_ref, s32[128,64]{1,0:T(8,128)} %fusion.op_ref, s32[128]{0:T(128)} %len_ref.3, f32[317,16,128]{2,1,0:T(8,128)} %pad.8.table_ref, ...), custom_call_target="tpu_custom_call" | custom-call | flops 4294967296 | bytes 4194304 | tf_op jit(solution)/shard_map/translate/pallas_call | solution.py:181
  68.5 1.2 collective-permute-start.13
  69.7 1.8 %collective-permute-start.14 = (f32[16,16,128]{2,1,0:T(8,128)}, f32[16,16,128]{2,1,0:T(8,128)S(1)}, u32[]{:S(2)}, u32[]{:S(2)}) collective-permute-start(f32[16,16,128]{2,1,0:T(8,128)} %get-tuple-element.60), channel_id=1, source_target_pairs={{0,24},{4,28},{8,16},{12,20},{16,8},{20,12},{24,0},{28,4},{1,25},{... | collective-permute-start | bytes 393224 | tf_op jit(solution)/shard_map/ppermute | solution.py:365
  71.5 1.4 %collective-permute-start.15 = (f32[16,16,128]{2,1,0:T(8,128)}, f32[16,16,128]{2,1,0:T(8,128)S(1)}, u32[]{:S(2)}, u32[]{:S(2)}) collective-permute-start(f32[16,16,128]{2,1,0:T(8,128)} %get-tuple-element.61), channel_id=1, source_target_pairs={{0,28},{4,24},{8,20},{12,16},{16,12},{20,8},{24,4},{28,0},{1,29},{... | collective-permute-start | bytes 393224 | tf_op jit(solution)/shard_map/ppermute | solution.py:365
  72.9 12.4 %translate.2 = (f32[16,16,128]{2,1,0:T(8,128)}, f32[16,16,128]{2,1,0:T(8,128)}, f32[16,16,128]{2,1,0:T(8,128)}, f32[16,16,128]{2,1,0:T(8,128)}) custom-call(s32[8]{0:T(128)} %broadcast_in_dim.14.me_ref, s32[128,64]{1,0:T(8,128)} %copy.12.partner_ref, s32[128,64]{1,0:T(8,128)} %fusion.op_ref, s32[128]{0:T(128)} %len_ref.3, f32[317,16,128]{2,1,0:T(8,128)} %pad.8.table_ref, ...), custom_call_target="tpu_custom_call" | custom-call | flops 4294967296 | bytes 4194304 | tf_op jit(solution)/shard_map/translate/pallas_call | solution.py:181
  85.3 0.0 collective-permute-done.12.rest_4_
  85.3 1.6 %collective-permute-start.10 = (f32[16,16,128]{2,1,0:T(8,128)}, f32[16,16,128]{2,1,0:T(8,128)S(1)}, u32[]{:S(2)}, u32[]{:S(2)}) collective-permute-start(f32[16,16,128]{2,1,0:T(8,128)} %get-tuple-element.56), channel_id=1, source_target_pairs={{0,8},{4,12},{8,0},{12,4},{16,24},{20,28},{24,16},{28,20},{1,9},{5... | collective-permute-start | bytes 393224 | tf_op jit(solution)/shard_map/ppermute | solution.py:365
  86.9 0.3 collective-permute-start.11
  87.2 4.8 %collective-permute-done.10.rest_2_ = f32[16,16,128]{2,1,0:T(8,128)S(1)} collective-permute-done((f32[16,16,128]{2,1,0:T(8,128)}, f32[16,16,128]{2,1,0:T(8,128)S(1)}, u32[]{:S(2)}, u32[]{:S(2)}) %collective-permute-start.10) | collective-permute-done | bytes 131104 | tf_op jit(solution)/shard_map/ppermute | solution.py:365
  92.0 1.7 %collective-permute-done.11.rest_3_ = f32[16,16,128]{2,1,0:T(8,128)S(1)} collective-permute-done((f32[16,16,128]{2,1,0:T(8,128)}, f32[16,16,128]{2,1,0:T(8,128)S(1)}, u32[]{:S(2)}, u32[]{:S(2)}) %collective-permute-start.11) | collective-permute-done | bytes 131104 | tf_op jit(solution)/shard_map/ppermute | solution.py:365
  93.7 0.6 copy-done.18
  94.3 20.4 %spread.1 = (f32[2,16,8192]{2,1,0:T(8,128)}, f32[2,128,4096]{2,1,0:T(8,128)}, f32[2,128,128]{2,1,0:T(8,128)}, f32[2,128,128]{2,1,0:T(8,128)}) custom-call(s32[8]{0:T(128)} %broadcast_in_dim.14.me_ref, f32[2,128,4096]{2,1,0:T(8,128)} %local_ref.1, f32[6,8192]{1,0:T(8,128)} %wn_ref.1, f32[6,8192]{1,0:T(8,128)} %wn_ref.1, ...), custom_call_target="tpu_custom_call" | custom-call | flops 8589934592 | bytes 12582912 | tf_op jit(solution)/shard_map/spread/pallas_call | solution.py:289
  114.8 0.1 collective-permute-start.16
  114.9 1.0 slice.65
  115.9 3.9 %collective-permute-start.17 = (f32[2,128,2]{2,1,0:T(8,128)S(1)}, f32[2,128,2]{2,1,0:T(8,128)S(1)}, u32[]{:S(2)}, u32[]{:S(2)}) collective-permute-start(f32[2,128,2]{2,1,0:T(8,128)S(1)} %slice.65), channel_id=1, source_target_pairs={{1,0},{2,1},{3,2},{0,3},{5,4},{6,5},{7,6},{4,7},{9,8},{10,9},{11,1... | collective-permute-start | bytes 6152 | tf_op jit(solution)/shard_map/ppermute | solution.py:393
  119.7 3.5 %collective-permute-done.16 = f32[2,128,3]{2,1,0:T(8,128)S(1)} collective-permute-done((f32[2,128,3]{2,1,0:T(8,128)}, f32[2,128,3]{2,1,0:T(8,128)S(1)}, u32[]{:S(2)}, u32[]{:S(2)}) %collective-permute-start.16) | collective-permute-done | bytes 3104 | tf_op jit(solution)/shard_map/ppermute | solution.py:392
  123.2 0.9 slice_add_fusion.1
  124.2 1.7 %scatter-add.6 = f32[2,128,4096]{2,1,0:T(8,128)} dynamic-update-slice(f32[2,128,4096]{2,1,0:T(8,128)} %get-tuple-element.63, f32[2,128,3]{2,1,0:T(8,128)S(1)} %slice_add_fusion.1, s32[]{:T(128)} %constant.67.clone.1, s32[]{:T(128)} %constant.67.clone.1, s32[]{:T(128)} %constant.67.clone.1) | dynamic-update-slice | bytes 6148 | tf_op jit(solution)/shard_map/scatter-add | solution.py:394
  125.8 1.0 slice_add_fusion
  126.9 1.8 %scatter-add.9 = f32[2,128,4096]{2,1,0:T(8,128)} dynamic-update-slice(f32[2,128,4096]{2,1,0:T(8,128)} %scatter-add.6, f32[2,128,2]{2,1,0:T(8,128)S(1)} %slice_add_fusion, s32[]{:T(128)} %constant.67.clone.1, s32[]{:T(128)} %constant.67.clone.1, s32[]{:T(128)} %constant.72.clone.1) | dynamic-update-slice | bytes 4100 | tf_op jit(solution)/shard_map/scatter-add | solution.py:395
  (49 shorter events, 0.1 us)
Async XLA Ops:
  0.6 12.3 %copy-start = (s32[128,64]{0,1:T(8,128)S(1)}, s32[128,64]{0,1:T(8,128)}, u32[]{:S(2)}) copy-start(s32[128,64]{0,1:T(8,128)} %param.17) | copy-start | bytes 98308
  0.6 13.0 %copy-start.1 = (s32[128,64]{0,1:T(8,128)S(1)}, s32[128,64]{0,1:T(8,128)}, u32[]{:S(2)}) copy-start(s32[128,64]{0,1:T(8,128)} %param.18) | copy-start | bytes 98308
  1.6 13.9 %collective-permute-start = (f32[2,128,3]{2,1,0:T(8,128)S(1)}, f32[2,128,3]{2,1,0:T(8,128)S(1)}, u32[]{:S(2)}, u32[]{:S(2)}) collective-permute-start(f32[2,128,3]{2,1,0:T(8,128)S(1)} %slice.60), channel_id=1, source_target_pairs={{1,0},{2,1},{3,2},{0,3},{5,4},{6,5},{7,6},{4,7},{9,8},{10,9},{11,1... | collective-permute-start | bytes 9224 | tf_op jit(solution)/shard_map/ppermute | solution.py:356
  7.7 7.8 %collective-permute-start.1 = (f32[2,128,2]{2,1,0:T(8,128)S(1)}, f32[2,128,2]{2,1,0:T(8,128)S(1)}, u32[]{:S(2)}, u32[]{:S(2)}) collective-permute-start(f32[2,128,2]{2,1,0:T(8,128)S(1)} %slice.61), channel_id=1, source_target_pairs={{0,1},{1,2},{2,3},{3,0},{4,5},{5,6},{6,7},{7,4},{8,9},{9,10},{10,1... | collective-permute-start | bytes 6152 | tf_op jit(solution)/shard_map/ppermute | solution.py:355
  24.6 13.2 %collective-permute-start.5 = (f32[16,16,128]{2,1,0:T(8,128)}, f32[16,16,128]{2,1,0:T(8,128)S(1)}, u32[]{:S(2)}, u32[]{:S(2)}) collective-permute-start(f32[16,16,128]{2,1,0:T(8,128)} %get-tuple-element.50), channel_id=1, source_target_pairs={{0,16},{4,20},{8,24},{12,28},{16,0},{20,4},{24,8},{28,12},{1,17},{... | collective-permute-start | bytes 393224 | tf_op jit(solution)/shard_map/ppermute | solution.py:365
  26.1 8.5 %copy-start.16 = (f32[16,16,128]{2,1,0:T(8,128)S(1)}, f32[16,16,128]{2,1,0:T(8,128)}, u32[]{:S(2)}) copy-start(f32[16,16,128]{2,1,0:T(8,128)} %get-tuple-element.52) | copy-start | bytes 393220
  26.1 10.3 %copy-start.14 = (f32[16,16,128]{2,1,0:T(8,128)S(1)}, f32[16,16,128]{2,1,0:T(8,128)}, u32[]{:S(2)}) copy-start(f32[16,16,128]{2,1,0:T(8,128)} %get-tuple-element.53) | copy-start | bytes 393220
  26.1 13.2 %copy-start.2 = (s32[128]{0:T(128)S(1)}, s32[128]{0:T(128)}, u32[]{:S(2)}) copy-start(s32[128]{0:T(128)} %len_ref.3) | copy-start | bytes 1540
  26.1 13.1 %collective-permute-start.6 = (f32[16,16,128]{2,1,0:T(8,128)}, f32[16,16,128]{2,1,0:T(8,128)S(1)}, u32[]{:S(2)}, u32[]{:S(2)}) collective-permute-start(f32[16,16,128]{2,1,0:T(8,128)} %get-tuple-element.51), channel_id=1, source_target_pairs={{0,20},{4,16},{8,28},{12,24},{16,4},{20,0},{24,12},{28,8},{1,21},{... | collective-permute-start | bytes 393224 | tf_op jit(solution)/shard_map/ppermute | solution.py:365
  34.6 7.3 %collective-permute-start.7 = (f32[16,16,128]{2,1,0:T(8,128)S(1)}, f32[16,16,128]{2,1,0:T(8,128)S(1)}, u32[]{:S(2)}, u32[]{:S(2)}) collective-permute-start(f32[16,16,128]{2,1,0:T(8,128)S(1)} %copy-done.16), channel_id=1, source_target_pairs={{0,24},{4,28},{8,16},{12,20},{16,8},{20,12},{24,0},{28,4},{1,25},{... | collective-permute-start | bytes 393224 | tf_op jit(solution)/shard_map/ppermute | solution.py:365
  36.4 7.4 %collective-permute-start.8 = (f32[16,16,128]{2,1,0:T(8,128)S(1)}, f32[16,16,128]{2,1,0:T(8,128)S(1)}, u32[]{:S(2)}, u32[]{:S(2)}) collective-permute-start(f32[16,16,128]{2,1,0:T(8,128)S(1)} %copy-done.14), channel_id=1, source_target_pairs={{0,28},{4,24},{8,20},{12,16},{16,12},{20,8},{24,4},{28,0},{1,29},{... | collective-permute-start | bytes 393224 | tf_op jit(solution)/shard_map/ppermute | solution.py:365
  37.4 6.4 %collective-permute-start.2 = (f32[16,16,128]{2,1,0:T(8,128)}, f32[16,16,128]{2,1,0:T(8,128)S(1)}, u32[]{:S(2)}, u32[]{:S(2)}) collective-permute-start(f32[16,16,128]{2,1,0:T(8,128)} %get-tuple-element.47), channel_id=1, source_target_pairs={{0,4},{4,0},{8,12},{12,8},{16,20},{20,16},{24,28},{28,24},{1,5},{5... | collective-permute-start | bytes 393224 | tf_op jit(solution)/shard_map/ppermute | solution.py:365
  37.7 12.5 %copy-start.3 = (f32[16,16,128]{2,1,0:T(8,128)}, f32[16,16,128]{2,1,0:T(8,128)S(1)}, u32[]{:S(2)}) copy-start(f32[16,16,128]{2,1,0:T(8,128)S(1)} %collective-permute-done.5.rest_4_) | copy-start | bytes 393220
  37.7 8.9 %collective-permute-start.3 = (f32[16,16,128]{2,1,0:T(8,128)}, f32[16,16,128]{2,1,0:T(8,128)S(1)}, u32[]{:S(2)}, u32[]{:S(2)}) collective-permute-start(f32[16,16,128]{2,1,0:T(8,128)} %get-tuple-element.48), channel_id=1, source_target_pairs={{0,8},{4,12},{8,0},{12,4},{16,24},{20,28},{24,16},{28,20},{1,9},{5... | collective-permute-start | bytes 393224 | tf_op jit(solution)/shard_map/ppermute | solution.py:365
  39.2 11.0 %copy-start.4 = (f32[16,16,128]{2,1,0:T(8,128)}, f32[16,16,128]{2,1,0:T(8,128)S(1)}, u32[]{:S(2)}) copy-start(f32[16,16,128]{2,1,0:T(8,128)S(1)} %collective-permute-done.6.rest_5_) | copy-start | bytes 393220
  39.2 10.4 %collective-permute-start.4 = (f32[16,16,128]{2,1,0:T(8,128)}, f32[16,16,128]{2,1,0:T(8,128)S(1)}, u32[]{:S(2)}, u32[]{:S(2)}) collective-permute-start(f32[16,16,128]{2,1,0:T(8,128)} %get-tuple-element.49), channel_id=1, source_target_pairs={{0,12},{4,8},{8,4},{12,0},{16,28},{20,24},{24,20},{28,16},{1,13},{... | collective-permute-start | bytes 393224 | tf_op jit(solution)/shard_map/ppermute | solution.py:365
  42.0 8.3 %copy-start.5 = (f32[16,16,128]{2,1,0:T(8,128)}, f32[16,16,128]{2,1,0:T(8,128)S(1)}, u32[]{:S(2)}) copy-start(f32[16,16,128]{2,1,0:T(8,128)S(1)} %collective-permute-done.7.rest_6_) | copy-start | bytes 393220
  43.8 6.4 %copy-start.6 = (f32[16,16,128]{2,1,0:T(8,128)}, f32[16,16,128]{2,1,0:T(8,128)S(1)}, u32[]{:S(2)}) copy-start(f32[16,16,128]{2,1,0:T(8,128)S(1)} %collective-permute-done.8.rest_7_) | copy-start | bytes 393220
  43.8 6.4 %copy-start.8 = (f32[16,16,128]{2,1,0:T(8,128)}, f32[16,16,128]{2,1,0:T(8,128)S(1)}, u32[]{:S(2)}) copy-start(f32[16,16,128]{2,1,0:T(8,128)S(1)} %collective-permute-done.2.rest_1_) | copy-start | bytes 393220
  46.6 3.6 %copy-start.11 = (f32[16,16,128]{2,1,0:T(8,128)}, f32[16,16,128]{2,1,0:T(8,128)S(1)}, u32[]{:S(2)}) copy-start(f32[16,16,128]{2,1,0:T(8,128)S(1)} %collective-permute-done.3.rest_2_) | copy-start | bytes 393220
  49.7 0.7 copy-start.13
  68.5 16.8 %collective-permute-start.12 = (f32[16,16,128]{2,1,0:T(8,128)}, f32[16,16,128]{2,1,0:T(8,128)S(1)}, u32[]{:S(2)}, u32[]{:S(2)}) collective-permute-start(f32[16,16,128]{2,1,0:T(8,128)} %get-tuple-element.58), channel_id=1, source_target_pairs={{0,16},{4,20},{8,24},{12,28},{16,0},{20,4},{24,8},{28,12},{1,17},{... | collective-permute-start | bytes 393224 | tf_op jit(solution)/shard_map/ppermute | solution.py:365
  68.5 18.3 %collective-permute-start.13 = (f32[16,16,128]{2,1,0:T(8,128)}, f32[16,16,128]{2,1,0:T(8,128)S(1)}, u32[]{:S(2)}, u32[]{:S(2)}) collective-permute-start(f32[16,16,128]{2,1,0:T(8,128)} %get-tuple-element.59), channel_id=1, source_target_pairs={{0,20},{4,16},{8,28},{12,24},{16,4},{20,0},{24,12},{28,8},{1,21},{... | collective-permute-start | bytes 393224 | tf_op jit(solution)/shard_map/ppermute | solution.py:365
  69.7 17.4 %collective-permute-start.14 = (f32[16,16,128]{2,1,0:T(8,128)}, f32[16,16,128]{2,1,0:T(8,128)S(1)}, u32[]{:S(2)}, u32[]{:S(2)}) collective-permute-start(f32[16,16,128]{2,1,0:T(8,128)} %get-tuple-element.60), channel_id=1, source_target_pairs={{0,24},{4,28},{8,16},{12,20},{16,8},{20,12},{24,0},{28,4},{1,25},{... | collective-permute-start | bytes 393224 | tf_op jit(solution)/shard_map/ppermute | solution.py:365
  71.5 15.7 %collective-permute-start.15 = (f32[16,16,128]{2,1,0:T(8,128)}, f32[16,16,128]{2,1,0:T(8,128)S(1)}, u32[]{:S(2)}, u32[]{:S(2)}) collective-permute-start(f32[16,16,128]{2,1,0:T(8,128)} %get-tuple-element.61), channel_id=1, source_target_pairs={{0,28},{4,24},{8,20},{12,16},{16,12},{20,8},{24,4},{28,0},{1,29},{... | collective-permute-start | bytes 393224 | tf_op jit(solution)/shard_map/ppermute | solution.py:365
  85.3 1.9 %collective-permute-start.9 = (f32[16,16,128]{2,1,0:T(8,128)}, f32[16,16,128]{2,1,0:T(8,128)S(1)}, u32[]{:S(2)}, u32[]{:S(2)}) collective-permute-start(f32[16,16,128]{2,1,0:T(8,128)} %get-tuple-element.55), channel_id=1, source_target_pairs={{0,4},{4,0},{8,12},{12,8},{16,20},{20,16},{24,28},{28,24},{1,5},{5... | collective-permute-start | bytes 393224 | tf_op jit(solution)/shard_map/ppermute | solution.py:365
  85.3 8.4 %copy-start.7 = (f32[16,16,128]{2,1,0:T(8,128)}, f32[16,16,128]{2,1,0:T(8,128)S(1)}, u32[]{:S(2)}) copy-start(f32[16,16,128]{2,1,0:T(8,128)S(1)} %collective-permute-done.12.rest_4_) | copy-start | bytes 393220
  85.3 6.6 %collective-permute-start.10 = (f32[16,16,128]{2,1,0:T(8,128)}, f32[16,16,128]{2,1,0:T(8,128)S(1)}, u32[]{:S(2)}, u32[]{:S(2)}) collective-permute-start(f32[16,16,128]{2,1,0:T(8,128)} %get-tuple-element.56), channel_id=1, source_target_pairs={{0,8},{4,12},{8,0},{12,4},{16,24},{20,28},{24,16},{28,20},{1,9},{5... | collective-permute-start | bytes 393224 | tf_op jit(solution)/shard_map/ppermute | solution.py:365
  86.9 6.8 %copy-start.9 = (f32[16,16,128]{2,1,0:T(8,128)}, f32[16,16,128]{2,1,0:T(8,128)S(1)}, u32[]{:S(2)}) copy-start(f32[16,16,128]{2,1,0:T(8,128)S(1)} %collective-permute-done.13.rest_5_) | copy-start | bytes 393220
  86.9 6.8 %collective-permute-start.11 = (f32[16,16,128]{2,1,0:T(8,128)}, f32[16,16,128]{2,1,0:T(8,128)S(1)}, u32[]{:S(2)}, u32[]{:S(2)}) collective-permute-start(f32[16,16,128]{2,1,0:T(8,128)} %get-tuple-element.57), channel_id=1, source_target_pairs={{0,12},{4,8},{8,4},{12,0},{16,28},{20,24},{24,20},{28,16},{1,13},{... | collective-permute-start | bytes 393224 | tf_op jit(solution)/shard_map/ppermute | solution.py:365
  87.2 6.5 %copy-start.10 = (f32[16,16,128]{2,1,0:T(8,128)}, f32[16,16,128]{2,1,0:T(8,128)S(1)}, u32[]{:S(2)}) copy-start(f32[16,16,128]{2,1,0:T(8,128)S(1)} %collective-permute-done.14.rest_6_) | copy-start | bytes 393220
  87.2 6.5 %copy-start.12 = (f32[16,16,128]{2,1,0:T(8,128)}, f32[16,16,128]{2,1,0:T(8,128)S(1)}, u32[]{:S(2)}) copy-start(f32[16,16,128]{2,1,0:T(8,128)S(1)} %collective-permute-done.15.rest_7_) | copy-start | bytes 393220
  87.2 6.5 %copy-start.15 = (f32[16,16,128]{2,1,0:T(8,128)}, f32[16,16,128]{2,1,0:T(8,128)S(1)}, u32[]{:S(2)}) copy-start(f32[16,16,128]{2,1,0:T(8,128)S(1)} %collective-permute-done.9.rest_1_) | copy-start | bytes 393220
  92.0 1.8 %copy-start.17 = (f32[16,16,128]{2,1,0:T(8,128)}, f32[16,16,128]{2,1,0:T(8,128)S(1)}, u32[]{:S(2)}) copy-start(f32[16,16,128]{2,1,0:T(8,128)S(1)} %collective-permute-done.10.rest_2_) | copy-start | bytes 393220
  93.7 0.7 copy-start.18
  114.8 8.4 %collective-permute-start.16 = (f32[2,128,3]{2,1,0:T(8,128)}, f32[2,128,3]{2,1,0:T(8,128)S(1)}, u32[]{:S(2)}, u32[]{:S(2)}) collective-permute-start(f32[2,128,3]{2,1,0:T(8,128)} %bitcast.8), channel_id=1, source_target_pairs={{0,1},{1,2},{2,3},{3,0},{4,5},{5,6},{6,7},{7,4},{8,9},{9,10},{10,1... | collective-permute-start | bytes 9224 | tf_op jit(solution)/shard_map/ppermute | solution.py:392
  115.9 10.0 %collective-permute-start.17 = (f32[2,128,2]{2,1,0:T(8,128)S(1)}, f32[2,128,2]{2,1,0:T(8,128)S(1)}, u32[]{:S(2)}, u32[]{:S(2)}) collective-permute-start(f32[2,128,2]{2,1,0:T(8,128)S(1)} %slice.65), channel_id=1, source_target_pairs={{1,0},{2,1},{3,2},{0,3},{5,4},{6,5},{7,6},{4,7},{9,8},{10,9},{11,1... | collective-permute-start | bytes 6152 | tf_op jit(solution)/shard_map/ppermute | solution.py:393

commit v2 on v0

--- a/solution.py
+++ b/solution.py
@@ -1,18 +1,632 @@
+import functools
+
 import jax
 import jax.numpy as jnp
 from jax import lax
+from jax.experimental import pallas as pl
+from jax.experimental.pallas import tpu as pltpu
 from jax.sharding import PartitionSpec as P
+
 
 TAPS = 6
 CHILDREN = 8
+LANES = 128
+RIM = TAPS // 2
+GROUP = 4
+UNROLL = 16
+GRANT = pltpu.CompilerParams(vmem_limit_bytes=12 << 20)
+
+
+def on_chip(*arrays):
+    return [pltpu.with_memory_space_constraint(array, pltpu.VMEM) for array in arrays]
+
+
+def split(values):
+    high = values.astype(jnp.bfloat16)
+    low = (values - high.astype(jnp.float32)).astype(jnp.bfloat16)
+    return high, low
+
+
+def contract(left, right, dims):
+    (lh, ll), (rh, rl) = left, right
+    axis_l, axis_r = dims
+    return lax.dot_general(
+        jnp.concatenate([lh, ll, lh], axis=axis_l),
+        jnp.concatenate([rh, rh, rl], axis=axis_r),
+        (((axis_l,), (axis_r,)), ((), ())),
+        preferred_element_type=jnp.float32,
+    )
+
+
+def turn(phase):
+    half = 0.5 * phase
+    square = half * half
+    sine = jnp.full_like(square, -1.0 / 39916800)
+    for term in (1.0 / 362880, -1.0 / 5040, 1.0 / 120, -1.0 / 6, 1.0):
+        sine = sine * square + term
+    sine = sine * half
+    cosine = jnp.full_like(square, 1.0 / 479001600)
+    for term in (-1.0 / 3628800, 1.0 / 40320, -1.0 / 720, 1.0 / 24, -0.5, 1.0):
+        cosine = cosine * square + term
+    double = sine + sine
+    return 1.0 - double * sine, double * cosine
+
+
+def tap_rows():
+    row = lax.broadcasted_iota(jnp.int32, (8, LANES), 0)
+    half = lax.broadcasted_iota(jnp.int32, (8, LANES), 1) // 2
+    near = row - half + (RIM - 1)
+    picks = []
+    for tile in range(-1, LANES // 16 + 1):
+        tap = near + 8 * tile
+        picks.append(jnp.where((tap >= 0) & (tap < TAPS), tap, TAPS))
+    return picks
+
+
+def band_tiles(weight, picks):
+    padded = jnp.concatenate([weight, jnp.zeros((8 - TAPS, LANES), jnp.float32)], axis=0)
+    return [
+        jnp.take_along_axis(padded, pick, axis=0, mode="promise_in_bounds") for pick in picks
+    ]
+
+
+def band(weight, picks):
+    high = weight.astype(jnp.bfloat16).astype(jnp.float32)
+    parts = []
+    zero = jnp.zeros((8, LANES), jnp.float32)
+    inner = LANES // 16
+    for piece in (high, weight - high):
+        first = band_tiles(piece[:, :LANES], picks)
+        second = band_tiles(piece[:, LANES:], picks)
+        left = first[1:] + [zero] * (inner - 1) + [zero] * (2 * inner - 1) + [first[0]]
+        right = [zero] * (inner - 1) + second[:-1] + [second[-1]] + [zero] * (2 * inner - 1)
+        columns = [jnp.concatenate(tiles, axis=0).astype(jnp.bfloat16) for tiles in (left, right)]
+        parts.append(jnp.concatenate(columns, axis=1))
+    return tuple(parts)
+
+
+def picker(first, rows):
+    row = lax.broadcasted_iota(jnp.int32, (rows, LANES), 0)
+    lane = lax.broadcasted_iota(jnp.int32, (rows, LANES), 1)
+    return (lane == row + first).astype(jnp.bfloat16)
+
+
+def merge(first, second, step, sub):
+    low = (sub & step) == 0
+    return jnp.where(low, first, second) + pltpu.roll(jnp.where(low, second, first), step, 0)
+
+
+def sublane_sums(blocks, sub):
+    for step in (1, 2, 4):
+        blocks = [merge(blocks[i], blocks[i + 1], step, sub) for i in range(0, len(blocks), 2)]
+    return blocks[0]
+
+
+def exchange(to_right, to_left):
+    forward, backward = ring(lax.axis_size("sample"))
+    from_left = lax.ppermute(to_right, "sample", forward)
+    from_right = lax.ppermute(to_left, "sample", backward)
+    return from_left, from_right
+
+
+def narrow(block, at):
+    pick = picker(at, 8)
+    high, low = split(block)
+    return lax.dot_general(
+        jnp.concatenate([pick, pick], axis=1),
+        jnp.concatenate([high, low], axis=1),
+        (((1,), (1,)), ((), ())),
+        preferred_element_type=jnp.float32,
+    )
+
+
+def rim_kernel(first_ref, last_ref, right_ref, left_ref):
+    rows = first_ref.shape[0] * first_ref.shape[1]
+    right_ref[...] = narrow(last_ref[...].reshape(rows, LANES), LANES - 8)
+    left_ref[...] = narrow(first_ref[...].reshape(rows, LANES), 0)
+
+
+def rims(child):
+    comps, children, width = child.shape
+    rows = comps * children
+    child = pltpu.with_memory_space_constraint(child, pltpu.HBM)
+    return pl.pallas_call(
+        rim_kernel,
+        grid=(1,),
+        in_specs=[
+            pl.BlockSpec((comps, children, LANES), lambda g: (0, 0, 0)),
+            pl.BlockSpec((comps, children, LANES), lambda g: (0, 0, width // LANES - 1)),
+        ],
+        out_specs=[pl.BlockSpec((8, rows), lambda g: (0, 0))] * 2,
+        out_shape=[jax.ShapeDtypeStruct((8, rows), jnp.float32)] * 2,
+        name="rims",
+        compiler_params=GRANT,
+        cost_estimate=pl.CostEstimate(flops=1 << 20, bytes_accessed=1 << 18, transcendentals=0),
+    )(child, child)
+
+
+def widen(compact, at):
+    high, low = split(compact)
+    pick = picker(at, 8)
+    return lax.dot_general(
+        jnp.concatenate([high, low], axis=0),
+        jnp.concatenate([pick, pick], axis=0),
+        (((0,), (0,)), ((), ())),
+        preferred_element_type=jnp.float32,
+    )
+
+
+def aggregate_kernel(me_ref, ks_ref, x_ref, before_ref, after_ref, w_ref, f_ref, *rest):
+    outs, (held, made_ref, even_ref, odd_ref, arrived) = rest[:-5], rest[-5:]
+    comps, children, width = x_ref.shape
+    rows = comps * children
+    parents = children // CHILDREN
+    total = me_ref.shape[0]
+    count = len(outs)
+    span = width // total
+    quads = span // (2 * LANES)
+    lane = lax.broadcasted_iota(jnp.int32, (rows, LANES), 1)
+    inner = lane < LANES // 2
+    sub = lax.broadcasted_iota(jnp.int32, (8, LANES), 0)
+    picks = tap_rows()
+
+    def copies(i):
+        piece = me_ref[0] ^ ks_ref[i]
+        left = jnp.maximum(piece * span - LANES, 0)
+        right = jnp.minimum(piece * span + span, width - LANES)
+        return [
+            pltpu.make_async_copy(
+                x_ref.at[:, :, pl.ds(pl.multiple_of(source, LANES), size)],
+                held.at[i, :, :, target : target + size],
+                arrived.at[i, j],
+            )
+            for j, (source, target, size) in enumerate(
+                ((left, 0, LANES), (piece * span, LANES, span), (right, LANES + span, LANES))
+            )
+        ]
+
+    for i in range(count):
+        for copy in copies(i):
+            copy.start()
+
+    def lanes_of(i, at):
+        return held[i, :, :, at * LANES : (at + 1) * LANES].reshape(rows, LANES)
+
+    def raise_quad(piece, i, quad, up_ref):
+        first = 2 * quad + 1
+        sides = split(jnp.where(inner, lanes_of(i, first + 2), lanes_of(i, first - 1)))
+        here = [split(lanes_of(i, first)), split(lanes_of(i, first + 1))]
+        rims = [
+            [jnp.where(inner, here[1][j], sides[j]) for j in range(2)],
+            [jnp.where(inner, sides[j], here[0][j]) for j in range(2)],
+        ]
+        for b in range(2):
+            left_hand = [jnp.concatenate([here[b][j], rims[b][j]], axis=1) for j in range(2)]
+            at = pl.multiple_of((piece * quads + quad) * 4 * LANES + b * 2 * LANES, 2 * LANES)
+            weight = w_ref[:, pl.ds(at, 2 * LANES)]
+            up_ref[:, 2 * LANES * b : 2 * LANES * (b + 1)] = contract(left_hand, band(weight, picks), (1, 0))
+
+    def sum_quad(piece, quad, slot, up_ref):
+        at = pl.multiple_of((piece * quads + quad) * 4 * LANES, 4 * LANES)
+        cosines, sines = turn(f_ref[:, pl.ds(at, 4 * LANES)])
+        for p in range(parents):
+            gathered = []
+            for b in range(4):
+                col = slice(LANES * b, LANES * (b + 1))
+                cosine, sine = cosines[:, col], sines[:, col]
+                real = up_ref[p * CHILDREN : (p + 1) * CHILDREN, col]
+                imag = up_ref[(parents + p) * CHILDREN : (parents + p + 1) * CHILDREN, col]
+                gathered.append(cosine * real - sine * imag)
+                gathered.append(cosine * imag + sine * real)
+            made_ref[slot, p, 8 * quad : 8 * quad + 8, :] = sublane_sums(gathered, sub)
+
+    ups = (even_ref, odd_ref)
+
+    def advance(i, carry):
+        piece = me_ref[0] ^ ks_ref[i]
+        earlier = jnp.maximum(i - 1, 0)
+        former = me_ref[0] ^ ks_ref[earlier]
+        for copy in copies(i):
+            copy.wait()
+
+        @pl.when(piece == 0)
+        def _():
+            held[i, :, :, :LANES] = widen(before_ref[...], LANES - 8).reshape(comps, children, LANES)
+
+        @pl.when(piece == total - 1)
+        def _():
+            held[i, :, :, LANES + span :] = widen(after_ref[...], 0).reshape(comps, children, LANES)
+
+        for quad in range(quads):
+            raise_quad(piece, i, quad, ups[quad % 2])
+            if quad:
+                sum_quad(piece, quad - 1, i, ups[(quad - 1) % 2])
+            else:
+                sum_quad(former, quads - 1, earlier, ups[1])
+        return carry
+
+    odd_ref[...] = jnp.zeros_like(odd_ref)
+    lax.fori_loop(0, count, advance, 0)
+    sum_quad(me_ref[0] ^ ks_ref[count - 1], quads - 1, count - 1, ups[1])
+    for i in range(count):
+        outs[i][...] = made_ref[i]
+
+
+def aggregate(me, total, ks, child, before, after, weight, phase):
+    count = len(ks)
+    comps, children, width = child.shape
+    parents = children // CHILDREN
+    rows = comps * children
+    span = width // total
+    rows_of = 4 * (span // LANES)
+    smem = pl.BlockSpec(memory_space=pltpu.SMEM)
+    vmem = pl.BlockSpec(memory_space=pltpu.VMEM)
+    return pl.pallas_call(
+        aggregate_kernel,
+        in_specs=[smem] * 2 + [pl.BlockSpec(memory_space=pl.ANY)] + [vmem] * 4,
+        out_specs=[vmem] * count,
+        out_shape=[jax.ShapeDtypeStruct((parents, rows_of, LANES), jnp.float32)] * count,
+        scratch_shapes=[
+            pltpu.VMEM((count, comps, children, span + 2 * LANES), jnp.float32),
+            pltpu.VMEM((count, parents, rows_of, LANES), jnp.float32),
+            pltpu.VMEM((rows, 4 * LANES), jnp.float32),
+            pltpu.VMEM((rows, 4 * LANES), jnp.float32),
+            pltpu.SemaphoreType.DMA((count, 3)),
+        ],
+        name="aggregate",
+        compiler_params=GRANT,
+        cost_estimate=pl.CostEstimate(flops=4 << 30, bytes_accessed=6 << 20, transcendentals=0),
+    )(
+        jnp.full((total,), me, jnp.int32),
+        jnp.array(ks, jnp.int32),
+        pltpu.with_memory_space_constraint(child, pltpu.HBM),
+        *on_chip(before, after, weight, phase),
+    )
+
+
+def place_kernel(me_ref, *rest):
+    total = me_ref.shape[0]
+    sources, held = rest[:total], rest[total]
+    parents, rows, _ = sources[0].shape
+    odd = (lax.broadcasted_iota(jnp.int32, (rows, LANES), 0) & 1) == 1
+    for k in range(total):
+        first = (me_ref[0] ^ k) * parents
+
+        def place(p, carry, k=k, first=first):
+            block = sources[k][p]
+            at = pl.multiple_of((first + p) * 2 * rows, 2 * rows)
+            held[pl.ds(at, rows), :] = block
+            held[pl.ds(at + rows, rows), :] = jnp.where(
+                odd, pltpu.roll(block, 1, 0), pltpu.roll(block, rows - 1, 0)
+            )
+            return carry
+
+        lax.fori_loop(0, parents, place, 0, unroll=4)
+
+
+def place(me, sources):
+    total = len(sources)
+    parents, rows, lanes = sources[0].shape
+    vmem = pl.BlockSpec(memory_space=pltpu.VMEM)
+    return pl.pallas_call(
+        place_kernel,
+        in_specs=[pl.BlockSpec(memory_space=pltpu.SMEM)] + [vmem] * total,
+        out_specs=vmem,
+        out_shape=jax.ShapeDtypeStruct((total * parents * 2 * rows, lanes), jnp.float32),
+        name="place",
+        compiler_params=GRANT,
+        cost_estimate=pl.CostEstimate(flops=1 << 20, bytes_accessed=3 << 20, transcendentals=0),
+    )(jnp.full((total,), me, jnp.int32), *on_chip(*sources))
+
+
+def translate_kernel(base, me_ref, ends_ref, at_ref, into_ref, keep_ref, partner_ref, op_ref, table_ref, held, *rest):
+    outs, sums = rest[:-1], rest[-1]
+    count = len(outs)
+    parents, rows, _ = outs[0].shape
+    table = table_ref.reshape(table_ref.shape[0] * rows, LANES)
+    odd = (lax.broadcasted_iota(jnp.int32, (rows, LANES), 0) & 1) == 1
+    part = ((me_ref[0] ^ base) // count) * count * parents
+    start = jnp.where(part > 0, ends_ref[jnp.maximum(part - 1, 0)], 0)
+    stop = ends_ref[part + count * parents - 1]
+    entries = at_ref.shape[0] - UNROLL + 1
+    slots = op_ref.shape[0] - GROUP + 1
+
+    def add(step, totals):
+        for group in range(UNROLL):
+            index = start + step * UNROLL
+            at = at_ref.at[pl.ds(group, entries)][index]
+            into = pl.multiple_of(into_ref.at[pl.ds(group, entries)][index], 2 * rows)
+            keep = keep_ref.at[pl.ds(group, entries)][index]
+            direct, crossed = [], []
+            for u in range(GROUP):
+                operator = table[pl.ds(pl.multiple_of(op_ref.at[pl.ds(u, slots)][at], rows), rows), :]
+                partner = pl.multiple_of(partner_ref.at[pl.ds(u, slots)][at], 2 * rows)
+                direct.append(operator * held[pl.ds(partner, rows), :])
+                crossed.append(operator * held[pl.ds(partner + rows, rows), :])
+            while len(direct) > 1:
+                direct = [a + b for a, b in zip(direct[::2], direct[1::2])]
+                crossed = [a + b for a, b in zip(crossed[::2], crossed[1::2])]
+            totals = (totals[0] * keep + direct[0], totals[1] * keep + crossed[0])
+            sums[pl.ds(into, rows), :] = totals[0]
+            sums[pl.ds(into + rows, rows), :] = totals[1]
+        return totals
+
+    zero = jnp.zeros((rows, LANES), jnp.float32)
+    lax.fori_loop(0, (stop - start + UNROLL - 1) // UNROLL, add, (zero, zero))
+    for k in range(count):
+        first = (me_ref[0] ^ (base + k)) * parents
+
+        def combine(q, carry, out_ref=outs[k], first=first):
+            at = pl.multiple_of((first + q) * 2 * rows, 2 * rows)
+            direct, crossed = sums[pl.ds(at, rows), :], sums[pl.ds(at + rows, rows), :]
+            real = direct - pltpu.roll(direct, rows - 1, 0)
+            imag = crossed + pltpu.roll(crossed, 1, 0)
+            out_ref[q] = jnp.where(odd, imag, real)
+            return carry
+
+        lax.fori_loop(0, parents, combine, 0, unroll=4)
+
+
+def plan(partners, operators, lengths, count, rows):
+    receivers, slots = operators.shape
+    rounds = (lengths + GROUP - 1) // GROUP
+    index = jnp.arange(receivers)
+    ends = jnp.sum(jnp.where(index[None, :] <= index[:, None], rounds[None, :], 0), axis=1)
+    group = jnp.arange(receivers * ((slots + GROUP - 1) // GROUP) + UNROLL)
+    passed = ends[None, :] <= group[:, None]
+    receiver = jnp.sum(passed.astype(jnp.int32), axis=1)
+    slot = (group - jnp.max(jnp.where(passed, ends[None, :], 0), axis=1)) * GROUP
+    alive = jnp.arange(slots)[None, :] < lengths[:, None]
+    operators = jnp.pad(jnp.where(alive, operators, count) * rows, ((0, 1), (0, 0)), constant_values=count * rows)
+    partners = jnp.pad(partners * (2 * rows), ((0, 1), (0, 0)))
+    return (
+        ends,
+        receiver * slots + slot,
+        receiver * (2 * rows),
+        (slot > 0).astype(jnp.float32),
+        partners.reshape(-1),
+        operators.reshape(-1),
+    )
+
+
+def translate(me, total, base, count, lists, table, held):
+    rows, lanes = table.shape[1:]
+    parents = held.shape[0] // (2 * rows * total)
+    smem = pl.BlockSpec(memory_space=pltpu.SMEM)
+    vmem = pl.BlockSpec(memory_space=pltpu.VMEM)
+    return pl.pallas_call(
+        functools.partial(translate_kernel, base),
+        in_specs=[smem] * (1 + len(lists)) + [vmem] * 2,
+        out_specs=[vmem] * count,
+        out_shape=[jax.ShapeDtypeStruct((parents, rows, lanes), jnp.float32)] * count,
+        scratch_shapes=[pltpu.VMEM(((total * parents + 1) * 2 * rows, lanes), jnp.float32)],
+        name="translate",
+        compiler_params=GRANT,
+        cost_estimate=pl.CostEstimate(flops=4 << 30, bytes_accessed=4 << 20, transcendentals=0),
+    )(jnp.full((total,), me, jnp.int32), *lists, *on_chip(table, held))
+
+
+def spread_kernel(me_ref, local_ref, w_ref, f_ref, *rest):
+    total = me_ref.shape[0]
+    sources = rest[:total]
+    incoming_ref, out_ref, low_ref, high_ref, fields, even, odd, mains, rim_ref = rest[total:]
+    stages = (even, odd)
+    parents, rows_of, _ = sources[0].shape
+    blocks = rows_of // 4
+    comps, children, _ = out_ref.shape
+    rows = comps * children
+    step = pl.program_id(0)
+    me = me_ref[0]
+    lane = lax.broadcasted_iota(jnp.int32, (rows, LANES), 1)
+    picks = tap_rows()
+    end = total * blocks - 1
+
+    def stage(index, b):
+        index = jnp.minimum(index, end)
+        piece = index // blocks
+        target = stages[b % 2]
+        at = pl.multiple_of(index * 2 * LANES, 2 * LANES)
+        cosines, sines = turn(f_ref[:, pl.ds(at, 2 * LANES)])
+        for half in range(2):
+            column = slice(LANES * half, LANES * (half + 1))
+            cosine, sine = cosines[:, column], sines[:, column]
+            row = 4 * (b % blocks) + 2 * half
+            for p in range(0, parents, 2):
+                reals, imags = [], []
+                for q in (p, p + 1):
+                    real = jnp.broadcast_to(fields[piece, pl.ds(q * rows_of + row, 1), :], (CHILDREN, LANES))
+                    imag = jnp.broadcast_to(fields[piece, pl.ds(q * rows_of + row + 1, 1), :], (CHILDREN, LANES))
+                    reals.append(cosine * real + sine * imag)
+                    imags.append(cosine * imag - sine * real)
+                for comp, pair in enumerate((reals, imags)):
+                    first = comp * children + p * CHILDREN
+                    high, low = split(jnp.concatenate(pair, axis=0))
+                    target[0, first : first + 2 * CHILDREN, column] = high
+                    target[1, first : first + 2 * CHILDREN, column] = low
+
+    def multiply(index, b):
+        at = pl.multiple_of(jnp.minimum(index, end) * 2 * LANES, 2 * LANES)
+        weight = w_ref[:, pl.ds(at, 2 * LANES)]
+        source = stages[b % 2]
+        both = contract((source[0], source[1]), band(weight, picks), (1, 1))
+        mains[b % 2] = both[:, :LANES]
+        rim_ref[b % 4] = both[:, LANES:]
+
+    @pl.when(step == 0)
+    def _():
+        for k in range(total):
+            fields[me ^ k] = sources[k][...].reshape(parents * rows_of, LANES)
+        stage(jnp.int32(0), 0)
+        multiply(jnp.int32(0), 0)
+        stage(jnp.int32(1), 1)
+        rim_ref[3] = jnp.zeros((rows, LANES), jnp.float32)
+        low_ref[...] = narrow(rim_ref[0], LANES - 8)
+
+    inside = jnp.where(step < total - 1, 1.0, 0.0).astype(jnp.float32)
+    first = step * blocks
+    for b in range(1, blocks + 1):
+        multiply(first + b, b)
+        stage(first + b + 1, b + 1)
+        columns = slice(LANES * (b - 1), LANES * b)
+        after = rim_ref[b % 4] * inside if b == blocks else rim_ref[b % 4]
+        value = mains[(b - 1) % 2] + jnp.where(lane < LANES // 2, rim_ref[(b - 2) % 4], after)
+        lanes = pl.ds(pl.multiple_of((first + b - 1) * LANES, LANES), LANES)
+        out_ref[:, :, columns] = local_ref[:, :, lanes] + value.reshape(comps, children, LANES)
+
+    for b in range(2 * blocks):
+        for comp in range(comps):
+            for part in range(parents // 8):
+                incoming_ref[comp, 8 * part : 8 * part + 8, b * LANES : (b + 1) * LANES] = fields[
+                    step, pl.ds(8 * part * rows_of + 2 * b + comp, 8, stride=rows_of), :
+                ]
+
+    @pl.when(step == total - 1)
+    def _():
+        high_ref[...] = narrow(rim_ref[(blocks - 1) % 4], 0)
+
+
+def spread(me, child_local, weight, phase, sources):
+    total = len(sources)
+    parents, rows_of, _ = sources[0].shape
+    comps, children, width = child_local.shape
+    rows = comps * children
+    span = width // total
+    smem = pl.BlockSpec(memory_space=pltpu.SMEM)
+    vmem = pl.BlockSpec(memory_space=pltpu.VMEM)
+    rim = pl.BlockSpec((8, rows), lambda g: (0, 0))
+    return pl.pallas_call(
+        spread_kernel,
+        grid=(total,),
+        in_specs=[smem] + [vmem] * (3 + total),
+        out_specs=[
+            pl.BlockSpec((comps, parents, 2 * span), lambda g: (0, 0, g)),
+            pl.BlockSpec((comps, children, span), lambda g: (0, 0, g)),
+            rim,
+            rim,
+        ],
+        out_shape=[
+            jax.ShapeDtypeStruct((comps, parents, 2 * width), jnp.float32),
+            jax.ShapeDtypeStruct((comps, children, width), jnp.float32),
+            jax.ShapeDtypeStruct((8, rows), jnp.float32),
+            jax.ShapeDtypeStruct((8, rows), jnp.float32),
+        ],
+        scratch_shapes=[
+            pltpu.VMEM((total, parents * rows_of, LANES), jnp.float32),
+            pltpu.VMEM((2, rows, 2 * LANES), jnp.bfloat16),
+            pltpu.VMEM((2, rows, 2 * LANES), jnp.bfloat16),
+            pltpu.VMEM((2, rows, LANES), jnp.float32),
+            pltpu.VMEM((4, rows, LANES), jnp.float32),
+        ],
+        name="spread",
+        compiler_params=GRANT,
+        cost_estimate=pl.CostEstimate(flops=8 << 30, bytes_accessed=12 << 20, transcendentals=0),
+    )(jnp.full((total,), me, jnp.int32), *on_chip(child_local, weight, phase, *sources))
+
+
+def join_kernel(from_left_ref, from_right_ref, whole_ref, out_ref, held, arrived, left):
+    del whole_ref
+    comps, children, width = out_ref.shape
+    ends = (0, width - LANES)
+    reads = [
+        pltpu.make_async_copy(out_ref.at[:, :, at : at + LANES], held.at[i], arrived.at[i])
+        for i, at in enumerate(ends)
+    ]
+    writes = [
+        pltpu.make_async_copy(held.at[i], out_ref.at[:, :, at : at + LANES], left.at[i])
+        for i, at in enumerate(ends)
+    ]
+    for read in reads:
+        read.start()
+    for i, (rim_ref, at) in enumerate(((from_left_ref, 0), (from_right_ref, LANES - 8))):
+        added = widen(rim_ref[...], at).reshape(comps, children, LANES)
+        reads[i].wait()
+        held[i] = held[i] + added
+        writes[i].start()
+    for write in writes:
+        write.wait()
+
+
+def join(child_incoming, from_left, from_right):
+    comps, children, _ = child_incoming.shape
+    whole = pl.BlockSpec(memory_space=pl.ANY)
+    return pl.pallas_call(
+        join_kernel,
+        in_specs=[pl.BlockSpec(memory_space=pltpu.VMEM)] * 2 + [whole],
+        out_specs=whole,
+        out_shape=jax.ShapeDtypeStruct(child_incoming.shape, jnp.float32),
+        input_output_aliases={2: 0},
+        scratch_shapes=[
+            pltpu.VMEM((2, comps, children, LANES), jnp.float32),
+            pltpu.SemaphoreType.DMA((2,)),
+            pltpu.SemaphoreType.DMA((2,)),
+        ],
+        name="join",
+        compiler_params=GRANT,
+        cost_estimate=pl.CostEstimate(flops=1 << 20, bytes_accessed=1 << 19, transcendentals=0),
+    )(*on_chip(from_left, from_right), child_incoming)
+
+
+def ring(count):
+    forward = [(i, (i + 1) % count) for i in range(count)]
+    return forward, [(target, source) for source, target in forward]
+
+
+def fast(
+    child_pattern,
+    child_local,
+    interp_weight,
+    child_phase,
+    translator,
+    partners,
+    operator_id,
+    list_len,
+):
+    total = lax.axis_size("cluster")
+    me = lax.axis_index("cluster")
+    before, after = exchange(*rims(child_pattern))
+
+    def swap(block, k):
+        if k == 0:
+            return block
+        return lax.ppermute(block, "cluster", [(i, i ^ k) for i in range(total)])
+
+    sent = [None] * total
+    for ks in gathers(total):
+        made = aggregate(me, total, ks, child_pattern, before, after, interp_weight, child_phase)
+        for k, block in zip(ks, made):
+            sent[k] = block
+    sources = [swap(sent[k], k) for k in range(total)]
+
+    translator, partners, operator_id, list_len, _ = lax.optimization_barrier(
+        (translator, partners, operator_id, list_len, sent[0])
+    )
+    count, comps, samples = translator.shape
+    table = translator.reshape(count, comps, samples // LANES, LANES).transpose(0, 2, 1, 3)
+    table = table.reshape(count, comps * samples // LANES, LANES)
+    rows = comps * samples // LANES // total
+    table = lax.dynamic_slice_in_dim(table, me * rows, rows, 1)
+    table = jnp.pad(table, ((0, 1), (0, 0), (0, 0)))
+    lists = plan(partners, operator_id, list_len, count, rows)
+    held = place(me, sources)
+    back = translate(me, total, 0, total, lists, table, held)
+    fields = [swap(back[k], k) for k in range(total)]
+    incoming, child_incoming, low, high = spread(
+        me, child_local, interp_weight, child_phase, fields
+    )
+    from_left, from_right = exchange(high, low)
+    return incoming, join(child_incoming, from_left, from_right)
+
+
+def gathers(total):
+    if total == 8:
+        return (7, 6, 5, 3), (2, 4, 1, 0)
+    order = tuple(range(total - 1, -1, -1))
+    return (order[: total // 2], order[total // 2 :])
 
 
 def with_halo(block, sides, width):
     for axis, dim in sides:
-        count = lax.axis_size(axis)
-        forward = [(i, i + 1) for i in range(count - 1)]
-        forward.append((count - 1, 0))
-        backward = [(target, source) for source, target in forward]
+        forward, backward = ring(lax.axis_size(axis))
         low = lax.ppermute(
             lax.slice_in_dim(block, block.shape[dim] - width, None, axis=dim), axis, forward
         )
@@ -21,7 +635,7 @@
     return block
 
 
-def translate(pattern, table, partner_rows, operator_rows, lengths):
+def translate_rows(pattern, table, partner_rows, operator_rows, lengths):
     receivers = partner_rows.shape[0]
     slot_count = partner_rows.shape[1]
     group_size = 16
@@ -57,7 +671,7 @@
     return jnp.stack([shifted_real, shifted_imag]).reshape(2, -1, incoming.shape[2])
 
 
-def local(
+def plain(
     child_pattern,
     child_local,
     interp_weight,
@@ -95,7 +709,7 @@
     own_partners = lax.dynamic_slice_in_dim(partners, first_row, parent_count, 0)
     own_operators = lax.dynamic_slice_in_dim(operator_id, first_row, parent_count, 0)
     own_lengths = lax.dynamic_slice_in_dim(list_len, first_row, parent_count, 0)
-    incoming = translate(whole, translator, own_partners, own_operators, own_lengths)
+    incoming = translate_rows(whole, translator, own_partners, own_operators, own_lengths)
     shift_even = phase_spread(incoming[:, :, 0::2], cos_even, sin_even)
     shift_odd = phase_spread(incoming[:, :, 1::2], cos_odd, sin_odd)
     weighted = jnp.stack(
@@ -111,6 +725,18 @@
         offset = 2 * rim_width - 1 - tap
         child_incoming = child_incoming + padded_weighted[tap, :, :, offset : offset + half_samples]
     return (incoming, child_incoming)
+
+
+def fits(width, total):
+    share = width // total
+    even = total > 1 and total & (total - 1) == 0 and share * total == width
+    return even and share >= 4 * LANES and share % (4 * LANES) == 0
+
+
+def local(child_pattern, *rest):
+    if fits(child_pattern.shape[2], lax.axis_size("cluster")):
+        return fast(child_pattern, *rest)
+    return plain(child_pattern, *rest)
 
 
 def solution(mesh):

time: 775 us -> 73 us (0.09); the launches traced: 766 us -> 72.8 us
  local copies, waits for them, and re-layouts: 401 us -> 2.49 us
  other arithmetic: 282 us -> 0.8 us
  waiting for transfers between devices: 59.1 us -> 18.4 us
  Pallas kernels: 0 us -> 29.2 us
  between operations: 14.8 us -> 0.88 us
  starting transfers between devices: 8.62 us -> 21 us
    gather x8 -> x0, local copies, waits for them, and re-layouts: 224 us -> none  [the longest x4 119 us: advance(): coupling = jnp.take(table, operator_cols, axis=0)]
    slice x18 -> x0, local copies, waits for them, and re-layouts: 151 us -> none  [the longest x4 84.2 us: advance(): real_part = jnp.sum(coup_real * source[0] - coup_imag * source[1], axis=1)]
    select_n x16 -> x1, other arithmetic: 124 us -> 0.01 us  [plan(): rounds = (lengths + GROUP - 1) // GROUP]
    reduce_sum x6 -> x1, other arithmetic: 99 us -> 0.1 us  [plan(): jnp.sum(jnp.where(index[None, :] <= index[:, None], rounds[None, :], 0),...]
    all_gather x1 -> x0, waiting for transfers between devices: 53.8 us -> none  [local(): whole = lax.all_gather(parent, 'cluster', axis=1, tiled=True)]
    add x13 -> x0, other arithmetic: 41.9 us -> none  [the longest x1 15.4 us: local(): child_incoming + padded_weighted[tap, :, :, offset:offset + half_samples]]
    pallas_call x0 -> x7, Pallas kernels: none -> 29.2 us  [the longest x2 9.94 us: aggregate(): pl.pallas_call(aggregate_kernel, in_specs=[smem] * 2 + [pl.BlockSpec(memo...]
    unnamed x7 -> x0, other arithmetic: 13.7 us -> none
  transfers between devices with their start and end apart: 5 -> 18, of which waited for: 3 -> 8; matrix products, arithmetic and copies ran while one was open for 5% -> 4% of each run, Pallas kernels for 0% -> 7%
where the time goes in v2:
time: 73 us; the launch traced here: 72.8 us
  Pallas kernels  29.2 us (40%)
  starting transfers between devices  21 us (29%)
  waiting for transfers between devices  18.4 us (25%)
  local copies, waits for them, and re-layouts  2.49 us (3%)
  between operations  0.88 us (1%)
  other arithmetic  0.8 us (1%)
    ppermute x14, waiting for transfers between devices, swap(): return lax.ppermute(block, 'cluster', [(i, i ^ k) for i in range(total)])  15.1 us
    ppermute x14, starting transfers between devices, swap(): return lax.ppermute(block, 'cluster', [(i, i ^ k) for i in range(total)])  12.1 us
    pallas_call x2, Pallas kernels, aggregate(): pl.pallas_call(aggregate_kernel, in_specs=[smem] * 2 + [pl.BlockSpec(memo...  9.94 us
    pallas_call x1, Pallas kernels, spread(): pl.pallas_call(spread_kernel, grid=(total,), in_specs=[smem] + [vmem] * (...  9.32 us
    pallas_call x1, Pallas kernels, translate(): pl.pallas_call(functools.partial(translate_kernel, base), in_specs=[smem]...  6.1 us
    ppermute x2, starting transfers between devices, exchange(): from_right = lax.ppermute(to_left, 'sample', backward)  4.5 us
    ppermute x2, starting transfers between devices, exchange(): from_left = lax.ppermute(to_right, 'sample', forward)  4.41 us
    ppermute x2, waiting for transfers between devices, exchange(): from_left = lax.ppermute(to_right, 'sample', forward)  3.34 us
  transfers between devices with their start and end apart: 18, of which 8 were waited for; matrix products, arithmetic and copies ran while one was open for 4% of the time, Pallas kernels for 7%

profile of v2, /device:TPU:0, one launch (start us, length us, event | category | flops | bytes accessed | tf_op | source)
XLA Modules:
  0.0 72.8 jit_solution(2567832279414424507)
XLA Ops:
  0.6 0.0 copy-start.4
  0.7 1.2 %rims.1 = (f32[8,256]{1,0:T(8,128)S(1)}, f32[8,256]{1,0:T(8,128)S(1)}) custom-call(f32[2,128,4096]{2,1,0:T(8,128)} %x_ref.3, f32[2,128,4096]{2,1,0:T(8,128)} %x_ref.3), custom_call_target="tpu_custom_call" | custom-call | flops 1048576 | bytes 262144 | tf_op jit(solution)/shard_map/rims/pallas_call | solution.py:133
  1.9 3.1 %collective-permute-start = (f32[8,256]{1,0:T(8,128)S(1)}, f32[8,256]{1,0:T(8,128)S(1)}, u32[]{:S(2)}, u32[]{:S(2)}) collective-permute-start(f32[8,256]{1,0:T(8,128)S(1)} %get-tuple-element.28), channel_id=1, source_target_pairs={{0,1},{1,2},{2,3},{3,0},{4,5},{5,6},{6,7},{7,4},{8,9},{9,10},{10,1... | collective-permute-start | bytes 24584 | tf_op jit(solution)/shard_map/ppermute | solution.py:107
  4.9 2.0 %collective-permute-start.1 = (f32[8,256]{1,0:T(8,128)S(1)}, f32[8,256]{1,0:T(8,128)S(1)}, u32[]{:S(2)}, u32[]{:S(2)}) collective-permute-start(f32[8,256]{1,0:T(8,128)S(1)} %get-tuple-element.29), channel_id=1, source_target_pairs={{1,0},{2,1},{3,2},{0,3},{5,4},{6,5},{7,6},{4,7},{9,8},{10,9},{11,1... | collective-permute-start | bytes 24584 | tf_op jit(solution)/shard_map/ppermute | solution.py:108
  7.0 1.7 %collective-permute-done.before_ref = f32[8,256]{1,0:T(8,128)S(1)} collective-permute-done((f32[8,256]{1,0:T(8,128)S(1)}, f32[8,256]{1,0:T(8,128)S(1)}, u32[]{:S(2)}, u32[]{:S(2)}) %collective-permute-start) | collective-permute-done | bytes 8224 | tf_op jit(solution)/shard_map/ppermute | solution.py:107
  8.7 0.0 collective-permute-done.1.after_ref
  8.7 0.0 copy-start.3
  8.7 5.0 %aggregate.3 = (f32[16,16,128]{2,1,0:T(8,128)S(1)}, f32[16,16,128]{2,1,0:T(8,128)S(1)}, f32[16,16,128]{2,1,0:T(8,128)S(1)}, f32[16,16,128]{2,1,0:T(8,128)S(1)}) custom-call(s32[8]{0:T(128)S(1)} %broadcast_in_dim.28.me_ref, s32[4]{0:T(128)S(1)} %copy-done.4, f32[2,128,4096]{2,1,0:T(8,128)} %x_ref.3, f32[8,256]{1,0:T(8,128)S(1)} %collective-permute-done.before_ref, ...), custom_call_target="tpu_custom_call" | custom-call | flops 4294967296 | bytes 6291456 | tf_op jit(solution)/shard_map/aggregate/pallas_call | solution.py:264
  13.7 0.1 collective-permute-start.4
  13.8 2.8 %collective-permute-start.6 = (f32[16,16,128]{2,1,0:T(8,128)S(1)}, f32[16,16,128]{2,1,0:T(8,128)S(1)}, u32[]{:S(2)}, u32[]{:S(2)}) collective-permute-start(f32[16,16,128]{2,1,0:T(8,128)S(1)} %get-tuple-element.39), channel_id=1, source_target_pairs={{0,20},{4,16},{8,28},{12,24},{16,4},{20,0},{24,12},{28,8},{1,21},{... | collective-permute-start | bytes 393224 | tf_op jit(solution)/shard_map/ppermute | solution.py:591
  16.6 0.3 collective-permute-start.7
  17.0 0.9 %collective-permute-start.8 = (f32[16,16,128]{2,1,0:T(8,128)S(1)}, f32[16,16,128]{2,1,0:T(8,128)S(1)}, u32[]{:S(2)}, u32[]{:S(2)}) collective-permute-start(f32[16,16,128]{2,1,0:T(8,128)S(1)} %get-tuple-element.41), channel_id=1, source_target_pairs={{0,28},{4,24},{8,20},{12,16},{16,12},{20,8},{24,4},{28,0},{1,29},{... | collective-permute-start | bytes 393224 | tf_op jit(solution)/shard_map/ppermute | solution.py:591
  17.9 5.0 %aggregate.2 = (f32[16,16,128]{2,1,0:T(8,128)S(1)}, f32[16,16,128]{2,1,0:T(8,128)S(1)}, f32[16,16,128]{2,1,0:T(8,128)S(1)}, f32[16,16,128]{2,1,0:T(8,128)S(1)}) custom-call(s32[8]{0:T(128)S(1)} %broadcast_in_dim.28.me_ref, s32[4]{0:T(128)S(1)} %copy-done.3, f32[2,128,4096]{2,1,0:T(8,128)} %x_ref.3, f32[8,256]{1,0:T(8,128)S(1)} %collective-permute-done.before_ref, ...), custom_call_target="tpu_custom_call" | custom-call | flops 4294967296 | bytes 6291456 | tf_op jit(solution)/shard_map/aggregate/pallas_call | solution.py:264
  22.9 0.1 select_reduce_fusion.1.ends_ref
  23.0 0.7 select_reduce_fusion
  23.7 0.1 copy.21
  23.8 0.1 reshape.20.op_ref
  23.9 0.1 copy.20
  24.0 0.1 reshape.19.partner_ref
  24.0 1.8 %collective-permute-start.2 = (f32[16,16,128]{2,1,0:T(8,128)S(1)}, f32[16,16,128]{2,1,0:T(8,128)S(1)}, u32[]{:S(2)}, u32[]{:S(2)}) collective-permute-start(f32[16,16,128]{2,1,0:T(8,128)S(1)} %get-tuple-element.35), channel_id=1, source_target_pairs={{0,4},{4,0},{8,12},{12,8},{16,20},{20,16},{24,28},{28,24},{1,5},{5... | collective-permute-start | bytes 393224 | tf_op jit(solution)/shard_map/ppermute | solution.py:591
  25.9 1.9 %constant_dynamic-slice_fusion = f32[316,16,128]{2,1,0:T(8,128)S(1)} fusion(f32[316,128,128]{2,1,0:T(8,128)} %bitcast.5, s32[]{:T(128)S(6)} %select_n.24), kind=kLoop, calls=%fused_computation.16 | loop fusion | bytes 5177348 | tf_op jit(solution)/shard_map/dynamic_slice | solution.py:607
  27.8 0.2 pad.13.table_ref
  28.0 0.0 collective-permute-done.4.rest_3_
  28.0 0.6 collective-permute-start.3
  28.6 0.4 collective-permute-start.5
  29.0 4.5 %collective-permute-done.3.rest_2_ = f32[16,16,128]{2,1,0:T(8,128)S(1)} collective-permute-done((f32[16,16,128]{2,1,0:T(8,128)S(1)}, f32[16,16,128]{2,1,0:T(8,128)S(1)}, u32[]{:S(2)}, u32[]{:S(2)}) %collective-permute-start.3) | collective-permute-done | bytes 131104 | tf_op jit(solution)/shard_map/ppermute | solution.py:591
  33.5 0.2 collective-permute-done.5.rest_4_
  33.7 0.8 %place.1.held = f32[4096,128]{1,0:T(8,128)S(1)} custom-call(s32[8]{0:T(128)S(1)} %broadcast_in_dim.28.me_ref, f32[16,16,128]{2,1,0:T(8,128)S(1)} %get-tuple-element.30.rest_0_, f32[16,16,128]{2,1,0:T(8,128)S(1)} %collective-permute-done.2.rest_1_, f32[16,16,128]{2,1,0:T(8,128)S(1)} %collective-permute-done.3.rest_2_, ...), custom_call_target="tpu_custom_call" | custom-call | flops 1048576 | bytes 3145728 | tf_op jit(solution)/shard_map/place/pallas_call | solution.py:311
  34.6 0.0 copy-start
  34.6 6.1 %translate.1 = (f32[16,16,128]{2,1,0:T(8,128)S(1)}, f32[16,16,128]{2,1,0:T(8,128)S(1)}, f32[16,16,128]{2,1,0:T(8,128)S(1)}, f32[16,16,128]{2,1,0:T(8,128)S(1)}, ...) custom-call(s32[8]{0:T(128)S(1)} %broadcast_in_dim.28.me_ref, ...), custom_call_target="tpu_custom_call" | custom-call | flops 4294967296 | bytes 4194304 | tf_op jit(solution)/shard_map/translate/pallas_call | solution.py:397
  40.7 0.1 collective-permute-start.9
  40.8 1.6 %collective-permute-start.10 = (f32[16,16,128]{2,1,0:T(8,128)S(1)}, f32[16,16,128]{2,1,0:T(8,128)S(1)}, u32[]{:S(2)}, u32[]{:S(2)}) collective-permute-start(f32[16,16,128]{2,1,0:T(8,128)S(1)} %get-tuple-element.44), channel_id=1, source_target_pairs={{0,8},{4,12},{8,0},{12,4},{16,24},{20,28},{24,16},{28,20},{1,9},{5... | collective-permute-start | bytes 393224 | tf_op jit(solution)/shard_map/ppermute | solution.py:591
  42.3 0.3 collective-permute-start.11
  42.6 0.4 collective-permute-start.12
  43.1 1.3 %collective-permute-start.13 = (f32[16,16,128]{2,1,0:T(8,128)S(1)}, f32[16,16,128]{2,1,0:T(8,128)S(1)}, u32[]{:S(2)}, u32[]{:S(2)}) collective-permute-start(f32[16,16,128]{2,1,0:T(8,128)S(1)} %get-tuple-element.47), channel_id=1, source_target_pairs={{0,20},{4,16},{8,28},{12,24},{16,4},{20,0},{24,12},{28,8},{1,21},{... | collective-permute-start | bytes 393224 | tf_op jit(solution)/shard_map/ppermute | solution.py:591
  44.3 0.0 collective-permute-done.9.rest_1_
  44.3 1.4 %collective-permute-start.14 = (f32[16,16,128]{2,1,0:T(8,128)S(1)}, f32[16,16,128]{2,1,0:T(8,128)S(1)}, u32[]{:S(2)}, u32[]{:S(2)}) collective-permute-start(f32[16,16,128]{2,1,0:T(8,128)S(1)} %get-tuple-element.48), channel_id=1, source_target_pairs={{0,24},{4,28},{8,16},{12,20},{16,8},{20,12},{24,0},{28,4},{1,25},{... | collective-permute-start | bytes 393224 | tf_op jit(solution)/shard_map/ppermute | solution.py:591
  45.8 1.4 %collective-permute-done.10.rest_2_ = f32[16,16,128]{2,1,0:T(8,128)S(1)} collective-permute-done((f32[16,16,128]{2,1,0:T(8,128)S(1)}, f32[16,16,128]{2,1,0:T(8,128)S(1)}, u32[]{:S(2)}, u32[]{:S(2)}) %collective-permute-start.10) | collective-permute-done | bytes 131104 | tf_op jit(solution)/shard_map/ppermute | solution.py:591
  47.2 0.1 collective-permute-start.15
  47.3 1.8 %collective-permute-done.11.rest_3_ = f32[16,16,128]{2,1,0:T(8,128)S(1)} collective-permute-done((f32[16,16,128]{2,1,0:T(8,128)S(1)}, f32[16,16,128]{2,1,0:T(8,128)S(1)}, u32[]{:S(2)}, u32[]{:S(2)}) %collective-permute-start.11) | collective-permute-done | bytes 131104 | tf_op jit(solution)/shard_map/ppermute | solution.py:591
  49.0 0.1 collective-permute-done.12.rest_4_
  49.1 7.0 %collective-permute-done.13.rest_5_ = f32[16,16,128]{2,1,0:T(8,128)S(1)} collective-permute-done((f32[16,16,128]{2,1,0:T(8,128)S(1)}, f32[16,16,128]{2,1,0:T(8,128)S(1)}, u32[]{:S(2)}, u32[]{:S(2)}) %collective-permute-start.13) | collective-permute-done | bytes 131104 | tf_op jit(solution)/shard_map/ppermute | solution.py:591
  56.2 0.0 collective-permute-done.14.rest_6_
  56.2 9.3 %spread.1 = (f32[2,16,8192]{2,1,0:T(8,128)}, f32[2,128,4096]{2,1,0:T(8,128)}, f32[8,256]{1,0:T(8,128)S(1)}, f32[8,256]{1,0:T(8,128)S(1)}) custom-call(s32[8]{0:T(128)S(1)} %broadcast_in_dim.28.me_ref, f32[2,128,4096]{2,1,0:T(8,128)S(1)} %copy-done, f32[6,8192]{1,0:T(8,128)S(1)} %copy-done.1, f32[8,8192]{1,0:T(8,128)S(1)} %copy-done.2, ...), custom_call_target="tpu_custom_call" | custom-call | flops 8589934592 | bytes 12582912 | tf_op jit(solution)/shard_map/spread/pallas_call | solution.py:497
  65.5 1.4 %collective-permute-start.16 = (f32[8,256]{1,0:T(8,128)S(1)}, f32[8,256]{1,0:T(8,128)S(1)}, u32[]{:S(2)}, u32[]{:S(2)}) collective-permute-start(f32[8,256]{1,0:T(8,128)S(1)} %get-tuple-element.51), channel_id=1, source_target_pairs={{0,1},{1,2},{2,3},{3,0},{4,5},{5,6},{6,7},{7,4},{8,9},{9,10},{10,1... | collective-permute-start | bytes 24584 | tf_op jit(solution)/shard_map/ppermute | solution.py:107
  66.9 2.5 %collective-permute-start.17 = (f32[8,256]{1,0:T(8,128)S(1)}, f32[8,256]{1,0:T(8,128)S(1)}, u32[]{:S(2)}, u32[]{:S(2)}) collective-permute-start(f32[8,256]{1,0:T(8,128)S(1)} %get-tuple-element.52), channel_id=1, source_target_pairs={{1,0},{2,1},{3,2},{0,3},{5,4},{6,5},{7,6},{4,7},{9,8},{10,9},{11,1... | collective-permute-start | bytes 24584 | tf_op jit(solution)/shard_map/ppermute | solution.py:108
  69.3 1.6 %collective-permute-done.16.from_left_ref = f32[8,256]{1,0:T(8,128)S(1)} collective-permute-done((f32[8,256]{1,0:T(8,128)S(1)}, f32[8,256]{1,0:T(8,128)S(1)}, u32[]{:S(2)}, u32[]{:S(2)}) %collective-permute-start.16) | collective-permute-done | bytes 8224 | tf_op jit(solution)/shard_map/ppermute | solution.py:107
  71.0 1.8 %join.1 = f32[2,128,4096]{2,1,0:T(8,128)} custom-call(f32[8,256]{1,0:T(8,128)S(1)} %collective-permute-done.16.from_left_ref, f32[8,256]{1,0:T(8,128)S(1)} %collective-permute-done.17.from_right_ref, f32[2,128,4096]{2,1,0:T(8,128)} %get-tuple-element.53.whole_ref), custom_call_target="tpu_custom_call", output_to_operand_aliasing={{}: (2, {})} | custom-call | flops 1048576 | bytes 524288 | tf_op jit(solution)/shard_map/join/pallas_call | solution.py:552
  (26 shorter events, 0.1 us)
Async XLA Ops:
  0.6 8.1 %copy-start.4 = (s32[4]{0:T(128)S(1)}, s32[4]{0:T(128)}, u32[]{:S(2)}) copy-start(s32[4]{0:T(128)} %constant.52.clone.ks_ref) | copy-start | bytes 52
  0.6 8.0 %copy-start.2 = (f32[8,8192]{1,0:T(8,128)S(1)}, f32[8,8192]{1,0:T(8,128)}, u32[]{:S(2)}) copy-start(f32[8,8192]{1,0:T(8,128)} %f_ref.5) | copy-start | bytes 786436
  0.7 8.0 %copy-start.1 = (f32[6,8192]{1,0:T(8,128)S(1)}, f32[6,8192]{1,0:T(8,128)}, u32[]{:S(2)}) copy-start(f32[6,8192]{1,0:T(8,128)} %w_ref.5) | copy-start | bytes 589828
  1.9 6.8 %collective-permute-start = (f32[8,256]{1,0:T(8,128)S(1)}, f32[8,256]{1,0:T(8,128)S(1)}, u32[]{:S(2)}, u32[]{:S(2)}) collective-permute-start(f32[8,256]{1,0:T(8,128)S(1)} %get-tuple-element.28), channel_id=1, source_target_pairs={{0,1},{1,2},{2,3},{3,0},{4,5},{5,6},{6,7},{7,4},{8,9},{9,10},{10,1... | collective-permute-start | bytes 24584 | tf_op jit(solution)/shard_map/ppermute | solution.py:107
  4.9 3.7 %collective-permute-start.1 = (f32[8,256]{1,0:T(8,128)S(1)}, f32[8,256]{1,0:T(8,128)S(1)}, u32[]{:S(2)}, u32[]{:S(2)}) collective-permute-start(f32[8,256]{1,0:T(8,128)S(1)} %get-tuple-element.29), channel_id=1, source_target_pairs={{1,0},{2,1},{3,2},{0,3},{5,4},{6,5},{7,6},{4,7},{9,8},{10,9},{11,1... | collective-permute-start | bytes 24584 | tf_op jit(solution)/shard_map/ppermute | solution.py:108
  8.7 9.2 %copy-start.3 = (s32[4]{0:T(128)S(1)}, s32[4]{0:T(128)}, u32[]{:S(2)}) copy-start(s32[4]{0:T(128)} %constant.53.clone.ks_ref) | copy-start | bytes 52
  13.7 14.3 %collective-permute-start.4 = (f32[16,16,128]{2,1,0:T(8,128)S(1)}, f32[16,16,128]{2,1,0:T(8,128)S(1)}, u32[]{:S(2)}, u32[]{:S(2)}) collective-permute-start(f32[16,16,128]{2,1,0:T(8,128)S(1)} %get-tuple-element.37), channel_id=1, source_target_pairs={{0,12},{4,8},{8,4},{12,0},{16,28},{20,24},{24,20},{28,16},{1,13},{... | collective-permute-start | bytes 393224 | tf_op jit(solution)/shard_map/ppermute | solution.py:591
  13.8 14.8 %collective-permute-start.6 = (f32[16,16,128]{2,1,0:T(8,128)S(1)}, f32[16,16,128]{2,1,0:T(8,128)S(1)}, u32[]{:S(2)}, u32[]{:S(2)}) collective-permute-start(f32[16,16,128]{2,1,0:T(8,128)S(1)} %get-tuple-element.39), channel_id=1, source_target_pairs={{0,20},{4,16},{8,28},{12,24},{16,4},{20,0},{24,12},{28,8},{1,21},{... | collective-permute-start | bytes 393224 | tf_op jit(solution)/shard_map/ppermute | solution.py:591
  16.6 12.4 %collective-permute-start.7 = (f32[16,16,128]{2,1,0:T(8,128)S(1)}, f32[16,16,128]{2,1,0:T(8,128)S(1)}, u32[]{:S(2)}, u32[]{:S(2)}) collective-permute-start(f32[16,16,128]{2,1,0:T(8,128)S(1)} %get-tuple-element.40), channel_id=1, source_target_pairs={{0,24},{4,28},{8,16},{12,20},{16,8},{20,12},{24,0},{28,4},{1,25},{... | collective-permute-start | bytes 393224 | tf_op jit(solution)/shard_map/ppermute | solution.py:591
  17.0 5.9 %copy-start.7 = (s32[128]{0:T(128)S(1)}, s32[128]{0:T(128)}, u32[]{:S(2)}) copy-start(s32[128]{0:T(128)} %param.17) | copy-start | bytes 1540
  17.0 6.7 %copy-start.5 = (s32[128,64]{0,1:T(8,128)S(1)}, s32[128,64]{0,1:T(8,128)}, u32[]{:S(2)}) copy-start(s32[128,64]{0,1:T(8,128)} %param.16) | copy-start | bytes 98308
  17.0 6.7 %copy-start.6 = (s32[128,64]{0,1:T(8,128)S(1)}, s32[128,64]{0,1:T(8,128)}, u32[]{:S(2)}) copy-start(s32[128,64]{0,1:T(8,128)} %param.15) | copy-start | bytes 98308
  17.0 12.0 %collective-permute-start.8 = (f32[16,16,128]{2,1,0:T(8,128)S(1)}, f32[16,16,128]{2,1,0:T(8,128)S(1)}, u32[]{:S(2)}, u32[]{:S(2)}) collective-permute-start(f32[16,16,128]{2,1,0:T(8,128)S(1)} %get-tuple-element.41), channel_id=1, source_target_pairs={{0,28},{4,24},{8,20},{12,16},{16,12},{20,8},{24,4},{28,0},{1,29},{... | collective-permute-start | bytes 393224 | tf_op jit(solution)/shard_map/ppermute | solution.py:591
  24.0 5.0 %collective-permute-start.2 = (f32[16,16,128]{2,1,0:T(8,128)S(1)}, f32[16,16,128]{2,1,0:T(8,128)S(1)}, u32[]{:S(2)}, u32[]{:S(2)}) collective-permute-start(f32[16,16,128]{2,1,0:T(8,128)S(1)} %get-tuple-element.35), channel_id=1, source_target_pairs={{0,4},{4,0},{8,12},{12,8},{16,20},{20,16},{24,28},{28,24},{1,5},{5... | collective-permute-start | bytes 393224 | tf_op jit(solution)/shard_map/ppermute | solution.py:591
  28.0 5.5 %collective-permute-start.3 = (f32[16,16,128]{2,1,0:T(8,128)S(1)}, f32[16,16,128]{2,1,0:T(8,128)S(1)}, u32[]{:S(2)}, u32[]{:S(2)}) collective-permute-start(f32[16,16,128]{2,1,0:T(8,128)S(1)} %get-tuple-element.36), channel_id=1, source_target_pairs={{0,8},{4,12},{8,0},{12,4},{16,24},{20,28},{24,16},{28,20},{1,9},{5... | collective-permute-start | bytes 393224 | tf_op jit(solution)/shard_map/ppermute | solution.py:591
  28.6 5.1 %collective-permute-start.5 = (f32[16,16,128]{2,1,0:T(8,128)S(1)}, f32[16,16,128]{2,1,0:T(8,128)S(1)}, u32[]{:S(2)}, u32[]{:S(2)}) collective-permute-start(f32[16,16,128]{2,1,0:T(8,128)S(1)} %get-tuple-element.38), channel_id=1, source_target_pairs={{0,16},{4,20},{8,24},{12,28},{16,0},{20,4},{24,8},{28,12},{1,17},{... | collective-permute-start | bytes 393224 | tf_op jit(solution)/shard_map/ppermute | solution.py:591
  34.6 21.6 %copy-start = (f32[2,128,4096]{2,1,0:T(8,128)S(1)}, f32[2,128,4096]{2,1,0:T(8,128)}, u32[]{:S(2)}) copy-start(f32[2,128,4096]{2,1,0:T(8,128)} %local_ref.1) | copy-start | bytes 12582916
  40.7 3.6 %collective-permute-start.9 = (f32[16,16,128]{2,1,0:T(8,128)S(1)}, f32[16,16,128]{2,1,0:T(8,128)S(1)}, u32[]{:S(2)}, u32[]{:S(2)}) collective-permute-start(f32[16,16,128]{2,1,0:T(8,128)S(1)} %get-tuple-element.43), channel_id=1, source_target_pairs={{0,4},{4,0},{8,12},{12,8},{16,20},{20,16},{24,28},{28,24},{1,5},{5... | collective-permute-start | bytes 393224 | tf_op jit(solution)/shard_map/ppermute | solution.py:591
  40.8 6.4 %collective-permute-start.10 = (f32[16,16,128]{2,1,0:T(8,128)S(1)}, f32[16,16,128]{2,1,0:T(8,128)S(1)}, u32[]{:S(2)}, u32[]{:S(2)}) collective-permute-start(f32[16,16,128]{2,1,0:T(8,128)S(1)} %get-tuple-element.44), channel_id=1, source_target_pairs={{0,8},{4,12},{8,0},{12,4},{16,24},{20,28},{24,16},{28,20},{1,9},{5... | collective-permute-start | bytes 393224 | tf_op jit(solution)/shard_map/ppermute | solution.py:591
  42.3 6.7 %collective-permute-start.11 = (f32[16,16,128]{2,1,0:T(8,128)S(1)}, f32[16,16,128]{2,1,0:T(8,128)S(1)}, u32[]{:S(2)}, u32[]{:S(2)}) collective-permute-start(f32[16,16,128]{2,1,0:T(8,128)S(1)} %get-tuple-element.45), channel_id=1, source_target_pairs={{0,12},{4,8},{8,4},{12,0},{16,28},{20,24},{24,20},{28,16},{1,13},{... | collective-permute-start | bytes 393224 | tf_op jit(solution)/shard_map/ppermute | solution.py:591
  42.6 6.5 %collective-permute-start.12 = (f32[16,16,128]{2,1,0:T(8,128)S(1)}, f32[16,16,128]{2,1,0:T(8,128)S(1)}, u32[]{:S(2)}, u32[]{:S(2)}) collective-permute-start(f32[16,16,128]{2,1,0:T(8,128)S(1)} %get-tuple-element.46), channel_id=1, source_target_pairs={{0,16},{4,20},{8,24},{12,28},{16,0},{20,4},{24,8},{28,12},{1,17},{... | collective-permute-start | bytes 393224 | tf_op jit(solution)/shard_map/ppermute | solution.py:591
  43.1 13.1 %collective-permute-start.13 = (f32[16,16,128]{2,1,0:T(8,128)S(1)}, f32[16,16,128]{2,1,0:T(8,128)S(1)}, u32[]{:S(2)}, u32[]{:S(2)}) collective-permute-start(f32[16,16,128]{2,1,0:T(8,128)S(1)} %get-tuple-element.47), channel_id=1, source_target_pairs={{0,20},{4,16},{8,28},{12,24},{16,4},{20,0},{24,12},{28,8},{1,21},{... | collective-permute-start | bytes 393224 | tf_op jit(solution)/shard_map/ppermute | solution.py:591
  44.3 11.9 %collective-permute-start.14 = (f32[16,16,128]{2,1,0:T(8,128)S(1)}, f32[16,16,128]{2,1,0:T(8,128)S(1)}, u32[]{:S(2)}, u32[]{:S(2)}) collective-permute-start(f32[16,16,128]{2,1,0:T(8,128)S(1)} %get-tuple-element.48), channel_id=1, source_target_pairs={{0,24},{4,28},{8,16},{12,20},{16,8},{20,12},{24,0},{28,4},{1,25},{... | collective-permute-start | bytes 393224 | tf_op jit(solution)/shard_map/ppermute | solution.py:591
  47.2 9.0 %collective-permute-start.15 = (f32[16,16,128]{2,1,0:T(8,128)S(1)}, f32[16,16,128]{2,1,0:T(8,128)S(1)}, u32[]{:S(2)}, u32[]{:S(2)}) collective-permute-start(f32[16,16,128]{2,1,0:T(8,128)S(1)} %get-tuple-element.49), channel_id=1, source_target_pairs={{0,28},{4,24},{8,20},{12,16},{16,12},{20,8},{24,4},{28,0},{1,29},{... | collective-permute-start | bytes 393224 | tf_op jit(solution)/shard_map/ppermute | solution.py:591
  65.5 5.5 %collective-permute-start.16 = (f32[8,256]{1,0:T(8,128)S(1)}, f32[8,256]{1,0:T(8,128)S(1)}, u32[]{:S(2)}, u32[]{:S(2)}) collective-permute-start(f32[8,256]{1,0:T(8,128)S(1)} %get-tuple-element.51), channel_id=1, source_target_pairs={{0,1},{1,2},{2,3},{3,0},{4,5},{5,6},{6,7},{7,4},{8,9},{9,10},{10,1... | collective-permute-start | bytes 24584 | tf_op jit(solution)/shard_map/ppermute | solution.py:107
  66.9 4.1 %collective-permute-start.17 = (f32[8,256]{1,0:T(8,128)S(1)}, f32[8,256]{1,0:T(8,128)S(1)}, u32[]{:S(2)}, u32[]{:S(2)}) collective-permute-start(f32[8,256]{1,0:T(8,128)S(1)} %get-tuple-element.52), channel_id=1, source_target_pairs={{1,0},{2,1},{3,2},{0,3},{5,4},{6,5},{7,6},{4,7},{9,8},{10,9},{11,1... | collective-permute-start | bytes 24584 | tf_op jit(solution)/shard_map/ppermute | solution.py:108

commit v3 on v2

--- a/solution.py
+++ b/solution.py
@@ -1,5 +1,3 @@
-import functools
-
 import jax
 import jax.numpy as jnp
 from jax import lax
@@ -284,10 +282,11 @@
     )
 
 
-def place_kernel(me_ref, *rest):
+def translate_kernel(me_ref, ends_ref, at_ref, into_ref, keep_ref, partner_ref, op_ref, table_ref, *rest):
     total = me_ref.shape[0]
-    sources, held = rest[:total], rest[total]
-    parents, rows, _ = sources[0].shape
+    sources, outs, (held, sums) = rest[:total], rest[total:-2], rest[-2:]
+    parents, rows, _ = outs[0].shape
+    table = table_ref.reshape(table_ref.shape[0] * rows, LANES)
     odd = (lax.broadcasted_iota(jnp.int32, (rows, LANES), 0) & 1) == 1
     for k in range(total):
         first = (me_ref[0] ^ k) * parents
@@ -303,37 +302,12 @@
 
         lax.fori_loop(0, parents, place, 0, unroll=4)
 
-
-def place(me, sources):
-    total = len(sources)
-    parents, rows, lanes = sources[0].shape
-    vmem = pl.BlockSpec(memory_space=pltpu.VMEM)
-    return pl.pallas_call(
-        place_kernel,
-        in_specs=[pl.BlockSpec(memory_space=pltpu.SMEM)] + [vmem] * total,
-        out_specs=vmem,
-        out_shape=jax.ShapeDtypeStruct((total * parents * 2 * rows, lanes), jnp.float32),
-        name="place",
-        compiler_params=GRANT,
-        cost_estimate=pl.CostEstimate(flops=1 << 20, bytes_accessed=3 << 20, transcendentals=0),
-    )(jnp.full((total,), me, jnp.int32), *on_chip(*sources))
-
-
-def translate_kernel(base, me_ref, ends_ref, at_ref, into_ref, keep_ref, partner_ref, op_ref, table_ref, held, *rest):
-    outs, sums = rest[:-1], rest[-1]
-    count = len(outs)
-    parents, rows, _ = outs[0].shape
-    table = table_ref.reshape(table_ref.shape[0] * rows, LANES)
-    odd = (lax.broadcasted_iota(jnp.int32, (rows, LANES), 0) & 1) == 1
-    part = ((me_ref[0] ^ base) // count) * count * parents
-    start = jnp.where(part > 0, ends_ref[jnp.maximum(part - 1, 0)], 0)
-    stop = ends_ref[part + count * parents - 1]
     entries = at_ref.shape[0] - UNROLL + 1
     slots = op_ref.shape[0] - GROUP + 1
 
     def add(step, totals):
         for group in range(UNROLL):
-            index = start + step * UNROLL
+            index = step * UNROLL
             at = at_ref.at[pl.ds(group, entries)][index]
             into = pl.multiple_of(into_ref.at[pl.ds(group, entries)][index], 2 * rows)
             keep = keep_ref.at[pl.ds(group, entries)][index]
@@ -352,9 +326,10 @@
         return totals
 
     zero = jnp.zeros((rows, LANES), jnp.float32)
-    lax.fori_loop(0, (stop - start + UNROLL - 1) // UNROLL, add, (zero, zero))
-    for k in range(count):
-        first = (me_ref[0] ^ (base + k)) * parents
+    groups = ends_ref[ends_ref.shape[0] - 1]
+    lax.fori_loop(0, (groups + UNROLL - 1) // UNROLL, add, (zero, zero))
+    for k in range(total):
+        first = (me_ref[0] ^ k) * parents
 
         def combine(q, carry, out_ref=outs[k], first=first):
             at = pl.multiple_of((first + q) * 2 * rows, 2 * rows)
@@ -389,21 +364,24 @@
     )
 
 
-def translate(me, total, base, count, lists, table, held):
-    rows, lanes = table.shape[1:]
-    parents = held.shape[0] // (2 * rows * total)
+def translate(me, lists, table, sources):
+    total = len(sources)
+    parents, rows, lanes = sources[0].shape
     smem = pl.BlockSpec(memory_space=pltpu.SMEM)
     vmem = pl.BlockSpec(memory_space=pltpu.VMEM)
     return pl.pallas_call(
-        functools.partial(translate_kernel, base),
-        in_specs=[smem] * (1 + len(lists)) + [vmem] * 2,
-        out_specs=[vmem] * count,
-        out_shape=[jax.ShapeDtypeStruct((parents, rows, lanes), jnp.float32)] * count,
-        scratch_shapes=[pltpu.VMEM(((total * parents + 1) * 2 * rows, lanes), jnp.float32)],
+        translate_kernel,
+        in_specs=[smem] * (1 + len(lists)) + [vmem] * (1 + total),
+        out_specs=[vmem] * total,
+        out_shape=[jax.ShapeDtypeStruct((parents, rows, lanes), jnp.float32)] * total,
+        scratch_shapes=[
+            pltpu.VMEM((total * parents * 2 * rows, lanes), jnp.float32),
+            pltpu.VMEM(((total * parents + 1) * 2 * rows, lanes), jnp.float32),
+        ],
         name="translate",
         compiler_params=GRANT,
         cost_estimate=pl.CostEstimate(flops=4 << 30, bytes_accessed=4 << 20, transcendentals=0),
-    )(jnp.full((total,), me, jnp.int32), *lists, *on_chip(table, held))
+    )(jnp.full((total,), me, jnp.int32), *lists, *on_chip(table, *sources))
 
 
 def spread_kernel(me_ref, local_ref, w_ref, f_ref, *rest):
@@ -431,24 +409,19 @@
             column = slice(LANES * half, LANES * (half + 1))
             cosine, sine = cosines[:, column], sines[:, column]
             row = 4 * (b % blocks) + 2 * half
-            for p in range(0, parents, 2):
-                reals, imags = [], []
-                for q in (p, p + 1):
-                    real = jnp.broadcast_to(fields[piece, pl.ds(q * rows_of + row, 1), :], (CHILDREN, LANES))
-                    imag = jnp.broadcast_to(fields[piece, pl.ds(q * rows_of + row + 1, 1), :], (CHILDREN, LANES))
-                    reals.append(cosine * real + sine * imag)
-                    imags.append(cosine * imag - sine * real)
-                for comp, pair in enumerate((reals, imags)):
-                    first = comp * children + p * CHILDREN
-                    high, low = split(jnp.concatenate(pair, axis=0))
-                    target[0, first : first + 2 * CHILDREN, column] = high
-                    target[1, first : first + 2 * CHILDREN, column] = low
+            for p in range(parents):
+                real = jnp.broadcast_to(fields[piece, pl.ds(p * rows_of + row, 1), :], (CHILDREN, LANES))
+                imag = jnp.broadcast_to(fields[piece, pl.ds(p * rows_of + row + 1, 1), :], (CHILDREN, LANES))
+                first = p * CHILDREN
+                target[first : first + CHILDREN, column] = cosine * real + sine * imag
+                first = first + children
+                target[first : first + CHILDREN, column] = cosine * imag - sine * real
 
     def multiply(index, b):
         at = pl.multiple_of(jnp.minimum(index, end) * 2 * LANES, 2 * LANES)
         weight = w_ref[:, pl.ds(at, 2 * LANES)]
         source = stages[b % 2]
-        both = contract((source[0], source[1]), band(weight, picks), (1, 1))
+        both = contract(split(source[...]), band(weight, picks), (1, 1))
         mains[b % 2] = both[:, :LANES]
         rim_ref[b % 4] = both[:, LANES:]
 
@@ -512,8 +485,8 @@
         ],
         scratch_shapes=[
             pltpu.VMEM((total, parents * rows_of, LANES), jnp.float32),
-            pltpu.VMEM((2, rows, 2 * LANES), jnp.bfloat16),
-            pltpu.VMEM((2, rows, 2 * LANES), jnp.bfloat16),
+            pltpu.VMEM((rows, 2 * LANES), jnp.float32),
+            pltpu.VMEM((rows, 2 * LANES), jnp.float32),
             pltpu.VMEM((2, rows, LANES), jnp.float32),
             pltpu.VMEM((4, rows, LANES), jnp.float32),
         ],
@@ -607,8 +580,7 @@
     table = lax.dynamic_slice_in_dim(table, me * rows, rows, 1)
     table = jnp.pad(table, ((0, 1), (0, 0), (0, 0)))
     lists = plan(partners, operator_id, list_len, count, rows)
-    held = place(me, sources)
-    back = translate(me, total, 0, total, lists, table, held)
+    back = translate(me, lists, table, sources)
     fields = [swap(back[k], k) for k in range(total)]
     incoming, child_incoming, low, high = spread(
         me, child_local, interp_weight, child_phase, fields

time: 73 us -> 71 us (0.973)
  Pallas kernels: 29.2 us -> 27.3 us
    pallas_call x1, Pallas kernels: 9.32 us -> 8.25 us  [spread(): pl.pallas_call(spread_kernel, grid=(total,), in_specs=[smem] + [vmem] * (...]
    pallas_call x2 -> x1, Pallas kernels: 6.91 us -> 6.04 us  [translate(): pl.pallas_call(translate_kernel, in_specs=[smem] * (1 + len(lists)) + [vm...]
  transfers between devices with their start and end apart: 18 -> 18, of which waited for: 8 -> 8; matrix products, arithmetic and copies ran while one was open for 4% -> 5% of each run, Pallas kernels for 7% -> 7%
where the time goes in v3:
time: 71 us; the launch traced here: 70.8 us
  Pallas kernels  27.3 us (38%)
  starting transfers between devices  21 us (30%)
  waiting for transfers between devices  18.4 us (26%)
  local copies, waits for them, and re-layouts  2.49 us (4%)
  between operations  0.86 us (1%)
  other arithmetic  0.8 us (1%)
    ppermute x14, waiting for transfers between devices, swap(): return lax.ppermute(block, 'cluster', [(i, i ^ k) for i in range(total)])  15.1 us
    ppermute x14, starting transfers between devices, swap(): return lax.ppermute(block, 'cluster', [(i, i ^ k) for i in range(total)])  12.1 us
    pallas_call x2, Pallas kernels, aggregate(): pl.pallas_call(aggregate_kernel, in_specs=[smem] * 2 + [pl.BlockSpec(memo...  9.94 us
    pallas_call x1, Pallas kernels, spread(): pl.pallas_call(spread_kernel, grid=(total,), in_specs=[smem] + [vmem] * (...  8.25 us
    pallas_call x1, Pallas kernels, translate(): pl.pallas_call(translate_kernel, in_specs=[smem] * (1 + len(lists)) + [vm...  6.04 us
    ppermute x2, starting transfers between devices, exchange(): from_right = lax.ppermute(to_left, 'sample', backward)  4.5 us
    ppermute x2, starting transfers between devices, exchange(): from_left = lax.ppermute(to_right, 'sample', forward)  4.41 us
    ppermute x2, waiting for transfers between devices, exchange(): from_left = lax.ppermute(to_right, 'sample', forward)  3.34 us
  transfers between devices with their start and end apart: 18, of which 8 were waited for; matrix products, arithmetic and copies ran while one was open for 5% of the time, Pallas kernels for 7%

profile of v3, /device:TPU:0, one launch (start us, length us, event | category | flops | bytes accessed | tf_op | source)
XLA Modules:
  0.0 70.8 jit_solution(13119935235850683285)
XLA Ops:
  0.6 0.0 copy-start.4
  0.7 1.2 %rims.1 = (f32[8,256]{1,0:T(8,128)S(1)}, f32[8,256]{1,0:T(8,128)S(1)}) custom-call(f32[2,128,4096]{2,1,0:T(8,128)} %x_ref.3, f32[2,128,4096]{2,1,0:T(8,128)} %x_ref.3), custom_call_target="tpu_custom_call" | custom-call | flops 1048576 | bytes 262144 | tf_op jit(solution)/shard_map/rims/pallas_call | solution.py:131
  1.9 3.1 %collective-permute-start = (f32[8,256]{1,0:T(8,128)S(1)}, f32[8,256]{1,0:T(8,128)S(1)}, u32[]{:S(2)}, u32[]{:S(2)}) collective-permute-start(f32[8,256]{1,0:T(8,128)S(1)} %get-tuple-element.28), channel_id=1, source_target_pairs={{0,1},{1,2},{2,3},{3,0},{4,5},{5,6},{6,7},{7,4},{8,9},{9,10},{10,1... | collective-permute-start | bytes 24584 | tf_op jit(solution)/shard_map/ppermute | solution.py:105
  4.9 2.0 %collective-permute-start.1 = (f32[8,256]{1,0:T(8,128)S(1)}, f32[8,256]{1,0:T(8,128)S(1)}, u32[]{:S(2)}, u32[]{:S(2)}) collective-permute-start(f32[8,256]{1,0:T(8,128)S(1)} %get-tuple-element.29), channel_id=1, source_target_pairs={{1,0},{2,1},{3,2},{0,3},{5,4},{6,5},{7,6},{4,7},{9,8},{10,9},{11,1... | collective-permute-start | bytes 24584 | tf_op jit(solution)/shard_map/ppermute | solution.py:106
  7.0 1.7 %collective-permute-done.before_ref = f32[8,256]{1,0:T(8,128)S(1)} collective-permute-done((f32[8,256]{1,0:T(8,128)S(1)}, f32[8,256]{1,0:T(8,128)S(1)}, u32[]{:S(2)}, u32[]{:S(2)}) %collective-permute-start) | collective-permute-done | bytes 8224 | tf_op jit(solution)/shard_map/ppermute | solution.py:105
  8.7 0.0 collective-permute-done.1.after_ref
  8.7 0.0 copy-start.3
  8.7 5.0 %aggregate.3 = (f32[16,16,128]{2,1,0:T(8,128)S(1)}, f32[16,16,128]{2,1,0:T(8,128)S(1)}, f32[16,16,128]{2,1,0:T(8,128)S(1)}, f32[16,16,128]{2,1,0:T(8,128)S(1)}) custom-call(s32[8]{0:T(128)S(1)} %broadcast_in_dim.28.me_ref, s32[4]{0:T(128)S(1)} %copy-done.4, f32[2,128,4096]{2,1,0:T(8,128)} %x_ref.3, f32[8,256]{1,0:T(8,128)S(1)} %collective-permute-done.before_ref, ...), custom_call_target="tpu_custom_call" | custom-call | flops 4294967296 | bytes 6291456 | tf_op jit(solution)/shard_map/aggregate/pallas_call | solution.py:262
  13.7 0.1 collective-permute-start.4
  13.8 2.8 %collective-permute-start.6 = (f32[16,16,128]{2,1,0:T(8,128)S(1)}, f32[16,16,128]{2,1,0:T(8,128)S(1)}, u32[]{:S(2)}, u32[]{:S(2)}) collective-permute-start(f32[16,16,128]{2,1,0:T(8,128)S(1)} %get-tuple-element.39), channel_id=1, source_target_pairs={{0,20},{4,16},{8,28},{12,24},{16,4},{20,0},{24,12},{28,8},{1,21},{... | collective-permute-start | bytes 393224 | tf_op jit(solution)/shard_map/ppermute | solution.py:564
  16.6 0.3 collective-permute-start.7
  17.0 0.9 %collective-permute-start.8 = (f32[16,16,128]{2,1,0:T(8,128)S(1)}, f32[16,16,128]{2,1,0:T(8,128)S(1)}, u32[]{:S(2)}, u32[]{:S(2)}) collective-permute-start(f32[16,16,128]{2,1,0:T(8,128)S(1)} %get-tuple-element.41), channel_id=1, source_target_pairs={{0,28},{4,24},{8,20},{12,16},{16,12},{20,8},{24,4},{28,0},{1,29},{... | collective-permute-start | bytes 393224 | tf_op jit(solution)/shard_map/ppermute | solution.py:564
  17.9 5.0 %aggregate.2 = (f32[16,16,128]{2,1,0:T(8,128)S(1)}, f32[16,16,128]{2,1,0:T(8,128)S(1)}, f32[16,16,128]{2,1,0:T(8,128)S(1)}, f32[16,16,128]{2,1,0:T(8,128)S(1)}) custom-call(s32[8]{0:T(128)S(1)} %broadcast_in_dim.28.me_ref, s32[4]{0:T(128)S(1)} %copy-done.3, f32[2,128,4096]{2,1,0:T(8,128)} %x_ref.3, f32[8,256]{1,0:T(8,128)S(1)} %collective-permute-done.before_ref, ...), custom_call_target="tpu_custom_call" | custom-call | flops 4294967296 | bytes 6291456 | tf_op jit(solution)/shard_map/aggregate/pallas_call | solution.py:262
  22.9 0.1 select_reduce_fusion.1.ends_ref
  23.0 0.7 select_reduce_fusion
  23.7 0.1 copy.21
  23.8 0.1 reshape.20.op_ref
  23.9 0.1 copy.20
  24.0 0.1 reshape.19.partner_ref
  24.0 1.8 %collective-permute-start.2 = (f32[16,16,128]{2,1,0:T(8,128)S(1)}, f32[16,16,128]{2,1,0:T(8,128)S(1)}, u32[]{:S(2)}, u32[]{:S(2)}) collective-permute-start(f32[16,16,128]{2,1,0:T(8,128)S(1)} %get-tuple-element.35), channel_id=1, source_target_pairs={{0,4},{4,0},{8,12},{12,8},{16,20},{20,16},{24,28},{28,24},{1,5},{5... | collective-permute-start | bytes 393224 | tf_op jit(solution)/shard_map/ppermute | solution.py:564
  25.9 1.9 %constant_dynamic-slice_fusion = f32[316,16,128]{2,1,0:T(8,128)S(1)} fusion(f32[316,128,128]{2,1,0:T(8,128)} %bitcast.5, s32[]{:T(128)S(6)} %select_n.24), kind=kLoop, calls=%fused_computation.16 | loop fusion | bytes 5177348 | tf_op jit(solution)/shard_map/dynamic_slice | solution.py:580
  27.8 0.2 pad.13.table_ref
  28.0 0.0 collective-permute-done.4.rest_3_
  28.0 0.6 collective-permute-start.3
  28.6 0.0 collective-permute-done.6.rest_5_
  28.6 0.4 collective-permute-start.5
  29.0 0.0 collective-permute-done.7.rest_6_
  29.0 0.0 collective-permute-done.8.rest_7_
  29.0 4.5 %collective-permute-done.3.rest_2_ = f32[16,16,128]{2,1,0:T(8,128)S(1)} collective-permute-done((f32[16,16,128]{2,1,0:T(8,128)S(1)}, f32[16,16,128]{2,1,0:T(8,128)S(1)}, u32[]{:S(2)}, u32[]{:S(2)}) %collective-permute-start.3) | collective-permute-done | bytes 131104 | tf_op jit(solution)/shard_map/ppermute | solution.py:564
  33.5 0.2 collective-permute-done.5.rest_4_
  33.7 6.0 %translate.1 = (f32[16,16,128]{2,1,0:T(8,128)S(1)}, f32[16,16,128]{2,1,0:T(8,128)S(1)}, f32[16,16,128]{2,1,0:T(8,128)S(1)}, f32[16,16,128]{2,1,0:T(8,128)S(1)}, ...) custom-call(s32[8]{0:T(128)S(1)} %broadcast_in_dim.28.me_ref, ...), custom_call_target="tpu_custom_call" | custom-call | flops 4294967296 | bytes 4194304 | tf_op jit(solution)/shard_map/translate/pallas_call | solution.py:372
  39.8 0.1 collective-permute-start.9
  39.9 1.6 %collective-permute-start.10 = (f32[16,16,128]{2,1,0:T(8,128)S(1)}, f32[16,16,128]{2,1,0:T(8,128)S(1)}, u32[]{:S(2)}, u32[]{:S(2)}) collective-permute-start(f32[16,16,128]{2,1,0:T(8,128)S(1)} %get-tuple-element.44), channel_id=1, source_target_pairs={{0,8},{4,12},{8,0},{12,4},{16,24},{20,28},{24,16},{28,20},{1,9},{5... | collective-permute-start | bytes 393224 | tf_op jit(solution)/shard_map/ppermute | solution.py:564
  41.5 0.3 collective-permute-start.11
  41.7 0.4 collective-permute-start.12
  42.2 1.3 %collective-permute-start.13 = (f32[16,16,128]{2,1,0:T(8,128)S(1)}, f32[16,16,128]{2,1,0:T(8,128)S(1)}, u32[]{:S(2)}, u32[]{:S(2)}) collective-permute-start(f32[16,16,128]{2,1,0:T(8,128)S(1)} %get-tuple-element.47), channel_id=1, source_target_pairs={{0,20},{4,16},{8,28},{12,24},{16,4},{20,0},{24,12},{28,8},{1,21},{... | collective-permute-start | bytes 393224 | tf_op jit(solution)/shard_map/ppermute | solution.py:564
  43.4 1.4 %collective-permute-start.14 = (f32[16,16,128]{2,1,0:T(8,128)S(1)}, f32[16,16,128]{2,1,0:T(8,128)S(1)}, u32[]{:S(2)}, u32[]{:S(2)}) collective-permute-start(f32[16,16,128]{2,1,0:T(8,128)S(1)} %get-tuple-element.48), channel_id=1, source_target_pairs={{0,24},{4,28},{8,16},{12,20},{16,8},{20,12},{24,0},{28,4},{1,25},{... | collective-permute-start | bytes 393224 | tf_op jit(solution)/shard_map/ppermute | solution.py:564
  44.9 1.4 %collective-permute-done.10.rest_2_ = f32[16,16,128]{2,1,0:T(8,128)S(1)} collective-permute-done((f32[16,16,128]{2,1,0:T(8,128)S(1)}, f32[16,16,128]{2,1,0:T(8,128)S(1)}, u32[]{:S(2)}, u32[]{:S(2)}) %collective-permute-start.10) | collective-permute-done | bytes 131104 | tf_op jit(solution)/shard_map/ppermute | solution.py:564
  46.3 0.1 collective-permute-start.15
  46.4 1.8 %collective-permute-done.11.rest_3_ = f32[16,16,128]{2,1,0:T(8,128)S(1)} collective-permute-done((f32[16,16,128]{2,1,0:T(8,128)S(1)}, f32[16,16,128]{2,1,0:T(8,128)S(1)}, u32[]{:S(2)}, u32[]{:S(2)}) %collective-permute-start.11) | collective-permute-done | bytes 131104 | tf_op jit(solution)/shard_map/ppermute | solution.py:564
  48.2 0.1 collective-permute-done.12.rest_4_
  48.3 7.0 %collective-permute-done.13.rest_5_ = f32[16,16,128]{2,1,0:T(8,128)S(1)} collective-permute-done((f32[16,16,128]{2,1,0:T(8,128)S(1)}, f32[16,16,128]{2,1,0:T(8,128)S(1)}, u32[]{:S(2)}, u32[]{:S(2)}) %collective-permute-start.13) | collective-permute-done | bytes 131104 | tf_op jit(solution)/shard_map/ppermute | solution.py:564
  55.3 8.3 %spread.1 = (f32[2,16,8192]{2,1,0:T(8,128)}, f32[2,128,4096]{2,1,0:T(8,128)}, f32[8,256]{1,0:T(8,128)S(1)}, f32[8,256]{1,0:T(8,128)S(1)}) custom-call(s32[8]{0:T(128)S(1)} %broadcast_in_dim.28.me_ref, f32[2,128,4096]{2,1,0:T(8,128)S(1)} %copy-done, f32[6,8192]{1,0:T(8,128)S(1)} %copy-done.1, f32[8,8192]{1,0:T(8,128)S(1)} %copy-done.2, ...), custom_call_target="tpu_custom_call" | custom-call | flops 8589934592 | bytes 12582912 | tf_op jit(solution)/shard_map/spread/pallas_call | solution.py:470
  63.6 1.4 %collective-permute-start.16 = (f32[8,256]{1,0:T(8,128)S(1)}, f32[8,256]{1,0:T(8,128)S(1)}, u32[]{:S(2)}, u32[]{:S(2)}) collective-permute-start(f32[8,256]{1,0:T(8,128)S(1)} %get-tuple-element.51), channel_id=1, source_target_pairs={{0,1},{1,2},{2,3},{3,0},{4,5},{5,6},{6,7},{7,4},{8,9},{9,10},{10,1... | collective-permute-start | bytes 24584 | tf_op jit(solution)/shard_map/ppermute | solution.py:105
  64.9 2.5 %collective-permute-start.17 = (f32[8,256]{1,0:T(8,128)S(1)}, f32[8,256]{1,0:T(8,128)S(1)}, u32[]{:S(2)}, u32[]{:S(2)}) collective-permute-start(f32[8,256]{1,0:T(8,128)S(1)} %get-tuple-element.52), channel_id=1, source_target_pairs={{1,0},{2,1},{3,2},{0,3},{5,4},{6,5},{7,6},{4,7},{9,8},{10,9},{11,1... | collective-permute-start | bytes 24584 | tf_op jit(solution)/shard_map/ppermute | solution.py:106
  67.4 1.6 %collective-permute-done.16.from_left_ref = f32[8,256]{1,0:T(8,128)S(1)} collective-permute-done((f32[8,256]{1,0:T(8,128)S(1)}, f32[8,256]{1,0:T(8,128)S(1)}, u32[]{:S(2)}, u32[]{:S(2)}) %collective-permute-start.16) | collective-permute-done | bytes 8224 | tf_op jit(solution)/shard_map/ppermute | solution.py:105
  69.0 0.0 collective-permute-done.17.from_right_ref
  69.0 1.8 %join.1 = f32[2,128,4096]{2,1,0:T(8,128)} custom-call(f32[8,256]{1,0:T(8,128)S(1)} %collective-permute-done.16.from_left_ref, f32[8,256]{1,0:T(8,128)S(1)} %collective-permute-done.17.from_right_ref, f32[2,128,4096]{2,1,0:T(8,128)} %get-tuple-element.53.whole_ref), custom_call_target="tpu_custom_call", output_to_operand_aliasing={{}: (2, {})} | custom-call | flops 1048576 | bytes 524288 | tf_op jit(solution)/shard_map/join/pallas_call | solution.py:525
  (25 shorter events, 0.1 us)
Async XLA Ops:
  0.6 8.1 %copy-start.4 = (s32[4]{0:T(128)S(1)}, s32[4]{0:T(128)}, u32[]{:S(2)}) copy-start(s32[4]{0:T(128)} %constant.52.clone.ks_ref) | copy-start | bytes 52
  0.6 8.0 %copy-start.2 = (f32[8,8192]{1,0:T(8,128)S(1)}, f32[8,8192]{1,0:T(8,128)}, u32[]{:S(2)}) copy-start(f32[8,8192]{1,0:T(8,128)} %f_ref.5) | copy-start | bytes 786436
  0.7 8.0 %copy-start.1 = (f32[6,8192]{1,0:T(8,128)S(1)}, f32[6,8192]{1,0:T(8,128)}, u32[]{:S(2)}) copy-start(f32[6,8192]{1,0:T(8,128)} %w_ref.5) | copy-start | bytes 589828
  1.9 6.8 %collective-permute-start = (f32[8,256]{1,0:T(8,128)S(1)}, f32[8,256]{1,0:T(8,128)S(1)}, u32[]{:S(2)}, u32[]{:S(2)}) collective-permute-start(f32[8,256]{1,0:T(8,128)S(1)} %get-tuple-element.28), channel_id=1, source_target_pairs={{0,1},{1,2},{2,3},{3,0},{4,5},{5,6},{6,7},{7,4},{8,9},{9,10},{10,1... | collective-permute-start | bytes 24584 | tf_op jit(solution)/shard_map/ppermute | solution.py:105
  4.9 3.7 %collective-permute-start.1 = (f32[8,256]{1,0:T(8,128)S(1)}, f32[8,256]{1,0:T(8,128)S(1)}, u32[]{:S(2)}, u32[]{:S(2)}) collective-permute-start(f32[8,256]{1,0:T(8,128)S(1)} %get-tuple-element.29), channel_id=1, source_target_pairs={{1,0},{2,1},{3,2},{0,3},{5,4},{6,5},{7,6},{4,7},{9,8},{10,9},{11,1... | collective-permute-start | bytes 24584 | tf_op jit(solution)/shard_map/ppermute | solution.py:106
  8.7 9.2 %copy-start.3 = (s32[4]{0:T(128)S(1)}, s32[4]{0:T(128)}, u32[]{:S(2)}) copy-start(s32[4]{0:T(128)} %constant.53.clone.ks_ref) | copy-start | bytes 52
  13.7 14.3 %collective-permute-start.4 = (f32[16,16,128]{2,1,0:T(8,128)S(1)}, f32[16,16,128]{2,1,0:T(8,128)S(1)}, u32[]{:S(2)}, u32[]{:S(2)}) collective-permute-start(f32[16,16,128]{2,1,0:T(8,128)S(1)} %get-tuple-element.37), channel_id=1, source_target_pairs={{0,12},{4,8},{8,4},{12,0},{16,28},{20,24},{24,20},{28,16},{1,13},{... | collective-permute-start | bytes 393224 | tf_op jit(solution)/shard_map/ppermute | solution.py:564
  13.8 14.8 %collective-permute-start.6 = (f32[16,16,128]{2,1,0:T(8,128)S(1)}, f32[16,16,128]{2,1,0:T(8,128)S(1)}, u32[]{:S(2)}, u32[]{:S(2)}) collective-permute-start(f32[16,16,128]{2,1,0:T(8,128)S(1)} %get-tuple-element.39), channel_id=1, source_target_pairs={{0,20},{4,16},{8,28},{12,24},{16,4},{20,0},{24,12},{28,8},{1,21},{... | collective-permute-start | bytes 393224 | tf_op jit(solution)/shard_map/ppermute | solution.py:564
  16.6 12.4 %collective-permute-start.7 = (f32[16,16,128]{2,1,0:T(8,128)S(1)}, f32[16,16,128]{2,1,0:T(8,128)S(1)}, u32[]{:S(2)}, u32[]{:S(2)}) collective-permute-start(f32[16,16,128]{2,1,0:T(8,128)S(1)} %get-tuple-element.40), channel_id=1, source_target_pairs={{0,24},{4,28},{8,16},{12,20},{16,8},{20,12},{24,0},{28,4},{1,25},{... | collective-permute-start | bytes 393224 | tf_op jit(solution)/shard_map/ppermute | solution.py:564
  17.0 5.9 %copy-start.7 = (s32[128]{0:T(128)S(1)}, s32[128]{0:T(128)}, u32[]{:S(2)}) copy-start(s32[128]{0:T(128)} %param.17) | copy-start | bytes 1540
  17.0 6.7 %copy-start.5 = (s32[128,64]{0,1:T(8,128)S(1)}, s32[128,64]{0,1:T(8,128)}, u32[]{:S(2)}) copy-start(s32[128,64]{0,1:T(8,128)} %param.16) | copy-start | bytes 98308
  17.0 6.7 %copy-start.6 = (s32[128,64]{0,1:T(8,128)S(1)}, s32[128,64]{0,1:T(8,128)}, u32[]{:S(2)}) copy-start(s32[128,64]{0,1:T(8,128)} %param.15) | copy-start | bytes 98308
  17.0 12.0 %collective-permute-start.8 = (f32[16,16,128]{2,1,0:T(8,128)S(1)}, f32[16,16,128]{2,1,0:T(8,128)S(1)}, u32[]{:S(2)}, u32[]{:S(2)}) collective-permute-start(f32[16,16,128]{2,1,0:T(8,128)S(1)} %get-tuple-element.41), channel_id=1, source_target_pairs={{0,28},{4,24},{8,20},{12,16},{16,12},{20,8},{24,4},{28,0},{1,29},{... | collective-permute-start | bytes 393224 | tf_op jit(solution)/shard_map/ppermute | solution.py:564
  24.0 5.0 %collective-permute-start.2 = (f32[16,16,128]{2,1,0:T(8,128)S(1)}, f32[16,16,128]{2,1,0:T(8,128)S(1)}, u32[]{:S(2)}, u32[]{:S(2)}) collective-permute-start(f32[16,16,128]{2,1,0:T(8,128)S(1)} %get-tuple-element.35), channel_id=1, source_target_pairs={{0,4},{4,0},{8,12},{12,8},{16,20},{20,16},{24,28},{28,24},{1,5},{5... | collective-permute-start | bytes 393224 | tf_op jit(solution)/shard_map/ppermute | solution.py:564
  28.0 5.5 %collective-permute-start.3 = (f32[16,16,128]{2,1,0:T(8,128)S(1)}, f32[16,16,128]{2,1,0:T(8,128)S(1)}, u32[]{:S(2)}, u32[]{:S(2)}) collective-permute-start(f32[16,16,128]{2,1,0:T(8,128)S(1)} %get-tuple-element.36), channel_id=1, source_target_pairs={{0,8},{4,12},{8,0},{12,4},{16,24},{20,28},{24,16},{28,20},{1,9},{5... | collective-permute-start | bytes 393224 | tf_op jit(solution)/shard_map/ppermute | solution.py:564
  28.6 5.1 %collective-permute-start.5 = (f32[16,16,128]{2,1,0:T(8,128)S(1)}, f32[16,16,128]{2,1,0:T(8,128)S(1)}, u32[]{:S(2)}, u32[]{:S(2)}) collective-permute-start(f32[16,16,128]{2,1,0:T(8,128)S(1)} %get-tuple-element.38), channel_id=1, source_target_pairs={{0,16},{4,20},{8,24},{12,28},{16,0},{20,4},{24,8},{28,12},{1,17},{... | collective-permute-start | bytes 393224 | tf_op jit(solution)/shard_map/ppermute | solution.py:564
  33.7 21.6 %copy-start = (f32[2,128,4096]{2,1,0:T(8,128)S(1)}, f32[2,128,4096]{2,1,0:T(8,128)}, u32[]{:S(2)}) copy-start(f32[2,128,4096]{2,1,0:T(8,128)} %local_ref.1) | copy-start | bytes 12582916
  39.8 3.6 %collective-permute-start.9 = (f32[16,16,128]{2,1,0:T(8,128)S(1)}, f32[16,16,128]{2,1,0:T(8,128)S(1)}, u32[]{:S(2)}, u32[]{:S(2)}) collective-permute-start(f32[16,16,128]{2,1,0:T(8,128)S(1)} %get-tuple-element.43), channel_id=1, source_target_pairs={{0,4},{4,0},{8,12},{12,8},{16,20},{20,16},{24,28},{28,24},{1,5},{5... | collective-permute-start | bytes 393224 | tf_op jit(solution)/shard_map/ppermute | solution.py:564
  39.9 6.4 %collective-permute-start.10 = (f32[16,16,128]{2,1,0:T(8,128)S(1)}, f32[16,16,128]{2,1,0:T(8,128)S(1)}, u32[]{:S(2)}, u32[]{:S(2)}) collective-permute-start(f32[16,16,128]{2,1,0:T(8,128)S(1)} %get-tuple-element.44), channel_id=1, source_target_pairs={{0,8},{4,12},{8,0},{12,4},{16,24},{20,28},{24,16},{28,20},{1,9},{5... | collective-permute-start | bytes 393224 | tf_op jit(solution)/shard_map/ppermute | solution.py:564
  41.5 6.7 %collective-permute-start.11 = (f32[16,16,128]{2,1,0:T(8,128)S(1)}, f32[16,16,128]{2,1,0:T(8,128)S(1)}, u32[]{:S(2)}, u32[]{:S(2)}) collective-permute-start(f32[16,16,128]{2,1,0:T(8,128)S(1)} %get-tuple-element.45), channel_id=1, source_target_pairs={{0,12},{4,8},{8,4},{12,0},{16,28},{20,24},{24,20},{28,16},{1,13},{... | collective-permute-start | bytes 393224 | tf_op jit(solution)/shard_map/ppermute | solution.py:564
  41.7 6.5 %collective-permute-start.12 = (f32[16,16,128]{2,1,0:T(8,128)S(1)}, f32[16,16,128]{2,1,0:T(8,128)S(1)}, u32[]{:S(2)}, u32[]{:S(2)}) collective-permute-start(f32[16,16,128]{2,1,0:T(8,128)S(1)} %get-tuple-element.46), channel_id=1, source_target_pairs={{0,16},{4,20},{8,24},{12,28},{16,0},{20,4},{24,8},{28,12},{1,17},{... | collective-permute-start | bytes 393224 | tf_op jit(solution)/shard_map/ppermute | solution.py:564
  42.2 13.1 %collective-permute-start.13 = (f32[16,16,128]{2,1,0:T(8,128)S(1)}, f32[16,16,128]{2,1,0:T(8,128)S(1)}, u32[]{:S(2)}, u32[]{:S(2)}) collective-permute-start(f32[16,16,128]{2,1,0:T(8,128)S(1)} %get-tuple-element.47), channel_id=1, source_target_pairs={{0,20},{4,16},{8,28},{12,24},{16,4},{20,0},{24,12},{28,8},{1,21},{... | collective-permute-start | bytes 393224 | tf_op jit(solution)/shard_map/ppermute | solution.py:564
  43.4 11.9 %collective-permute-start.14 = (f32[16,16,128]{2,1,0:T(8,128)S(1)}, f32[16,16,128]{2,1,0:T(8,128)S(1)}, u32[]{:S(2)}, u32[]{:S(2)}) collective-permute-start(f32[16,16,128]{2,1,0:T(8,128)S(1)} %get-tuple-element.48), channel_id=1, source_target_pairs={{0,24},{4,28},{8,16},{12,20},{16,8},{20,12},{24,0},{28,4},{1,25},{... | collective-permute-start | bytes 393224 | tf_op jit(solution)/shard_map/ppermute | solution.py:564
  46.3 9.0 %collective-permute-start.15 = (f32[16,16,128]{2,1,0:T(8,128)S(1)}, f32[16,16,128]{2,1,0:T(8,128)S(1)}, u32[]{:S(2)}, u32[]{:S(2)}) collective-permute-start(f32[16,16,128]{2,1,0:T(8,128)S(1)} %get-tuple-element.49), channel_id=1, source_target_pairs={{0,28},{4,24},{8,20},{12,16},{16,12},{20,8},{24,4},{28,0},{1,29},{... | collective-permute-start | bytes 393224 | tf_op jit(solution)/shard_map/ppermute | solution.py:564
  63.6 5.5 %collective-permute-start.16 = (f32[8,256]{1,0:T(8,128)S(1)}, f32[8,256]{1,0:T(8,128)S(1)}, u32[]{:S(2)}, u32[]{:S(2)}) collective-permute-start(f32[8,256]{1,0:T(8,128)S(1)} %get-tuple-element.51), channel_id=1, source_target_pairs={{0,1},{1,2},{2,3},{3,0},{4,5},{5,6},{6,7},{7,4},{8,9},{9,10},{10,1... | collective-permute-start | bytes 24584 | tf_op jit(solution)/shard_map/ppermute | solution.py:105
  64.9 4.1 %collective-permute-start.17 = (f32[8,256]{1,0:T(8,128)S(1)}, f32[8,256]{1,0:T(8,128)S(1)}, u32[]{:S(2)}, u32[]{:S(2)}) collective-permute-start(f32[8,256]{1,0:T(8,128)S(1)} %get-tuple-element.52), channel_id=1, source_target_pairs={{1,0},{2,1},{3,2},{0,3},{5,4},{6,5},{7,6},{4,7},{9,8},{10,9},{11,1... | collective-permute-start | bytes 24584 | tf_op jit(solution)/shard_map/ppermute | solution.py:106
